TPU v7x, 128 devices: a whole 4x4x4 slice. The times are simulated.
128 devices in a mesh: row: 16 (over y, z), col: 8 (over x, core).
Axes of the slice: x: 4, y: 4, z: 4, core: 2. Of those that a mesh axis runs over, the one named last changes fastest.
Arguments:
- init_mean: float32 [256], replicated, may hold values from -6 to 6
- init_var: float32 [256], replicated, may hold values from 0.1 to 2
- decay: float32 [4096, 256], P(('row', 'col')), may hold values from 0 to 1
- coupling: bfloat16 [4096, 256, 256], P(('row', 'col')), may hold values from -0.0234375 to 0.0234375
- obs_map: bfloat16 [4096, 64, 256], P(('row', 'col')), may hold values from -0.375 to 0.375
- gain: bfloat16 [4096, 64, 256], P(('row', 'col')), may hold values from -0.0625 to 0.0625
- noise_factor: bfloat16 [256, 256], replicated, may hold values from -0.02734375 to 0.02734375
- obs_var: float32 [64], replicated, may hold values from 0.25 to 4
- observed: float32 [4096, 64], P(('row', 'col')), may hold values from -6 to 6
Outputs:
- means: float32 [4096, 256], P(('row', 'col'))
- variances: float32 [4096, 256], P(('row', 'col'))
All inputs are finite; a program needn't handle non-finite values.
Results may differ from a plain program's by a relative error of at most 0.00037.
Values sent between devices are 32-bit elements; how exact they have to be, the bound alone decides.
A program may use at most 128 MiB of HBM per device.

v0:
```python
import jax
import jax.numpy as jnp
from jax import lax
from jax.sharding import PartitionSpec as P

highest = lax.Precision.HIGHEST


def entering(shard, axis, combine, identity):
    size, place = (lax.axis_size(axis), lax.axis_index(axis))
    everything = jax.tree.map(lambda part: lax.all_gather(part, axis), shard)
    start = jax.tree.map(
        lambda part, zero: jnp.broadcast_to(jnp.asarray(zero, part.dtype), part.shape),
        shard,
        identity,
    )

    def hop(k, before):
        reached = k < place
        new = combine(before, jax.tree.map(lambda part: part[k], everything))
        return jax.tree.map(lambda a, b: jnp.where(reached, a, b), new, before)

    return lax.fori_loop(0, size, hop, start)


def broadcast(block, axis, holder):
    block = jnp.where(lax.axis_index(axis) == holder, block, jnp.zeros_like(block))
    return lax.psum(block, axis)


def combine(earlier, later):
    earlier_map, earlier_shift, earlier_noise = earlier
    later_map, later_shift, later_noise = later
    joined_map = jnp.matmul(later_map, earlier_map, precision=highest)
    joined_shift = (
        jnp.einsum("...ij,...j->...i", later_map, earlier_shift, precision=highest) + later_shift
    )
    moved = jnp.matmul(later_map, earlier_noise, precision=highest)
    joined_noise = (
        jnp.matmul(moved, jnp.swapaxes(later_map, -1, -2), precision=highest) + later_noise
    )
    return (joined_map, joined_shift, joined_noise)


def build_steps(decay, coupling, obs_map, gain, noise_factor, obs_var, observed):
    width = decay.shape[1]
    unit = jnp.eye(width, dtype=jnp.float32)
    trans = unit[None] * decay[:, None, :] + coupling.astype(jnp.float32)
    obs_f = obs_map.astype(jnp.float32) * decay[:, None, :] + jnp.einsum(
        "tms,tsr->tmr", obs_map, coupling, preferred_element_type=jnp.float32
    )
    obs_f = obs_f.astype(jnp.bfloat16)
    step_map = trans - jnp.einsum("tms,tmr->tsr", gain, obs_f, preferred_element_type=jnp.float32)
    obs_g = jnp.einsum(
        "tms,sr->tmr", obs_map, noise_factor, preferred_element_type=jnp.float32
    ).astype(jnp.bfloat16)
    shaped = noise_factor.astype(jnp.float32)[None] - jnp.einsum(
        "tms,tmr->tsr", gain, obs_g, preferred_element_type=jnp.float32
    )
    shaped = shaped.astype(jnp.bfloat16)
    weighted = (gain.astype(jnp.float32) * obs_var[None, :, None]).astype(jnp.bfloat16)
    noise = jnp.einsum("tsr,tqr->tsq", shaped, shaped, preferred_element_type=jnp.float32)
    noise = noise + jnp.einsum("tms,tmq->tsq", gain, weighted, preferred_element_type=jnp.float32)
    shift = jnp.einsum("tm,tms->ts", observed, gain.astype(jnp.float32), precision=highest)
    return (step_map, shift, noise)


def per_device(
    init_mean, init_var, decay, coupling, obs_map, gain, noise_factor, obs_var, observed
):
    width = decay.shape[1]
    step_map, shift, noise = build_steps(
        decay, coupling, obs_map, gain, noise_factor, obs_var, observed
    )
    neutral = (
        jnp.eye(width, dtype=jnp.float32),
        jnp.zeros((width,), jnp.float32),
        jnp.zeros((width, width), jnp.float32),
    )

    def accumulate_total(carry, element):
        return (combine(carry, element), None)

    total, _ = lax.scan(accumulate_total, neutral, (step_map, shift, noise))
    inner = entering(total, "col", combine, neutral)
    row_whole = combine(inner, total)
    row_total = (
        broadcast(row_whole[0], "col", lax.axis_size("col") - 1),
        broadcast(row_whole[1], "col", lax.axis_size("col") - 1),
        broadcast(row_whole[2], "col", lax.axis_size("col") - 1),
    )
    outer = entering(row_total, "row", combine, neutral)
    before = combine(outer, inner)
    carry_map, carry_shift, carry_noise = before
    entry_mean = jnp.dot(carry_map, init_mean, precision=highest) + carry_shift
    entry_cov = jnp.dot(carry_map * init_var[None, :], carry_map.T, precision=highest) + carry_noise

    def advance(state, element):
        state_mean, state_cov = state
        element_map, element_shift, element_noise = element
        state_mean = jnp.dot(element_map, state_mean, precision=highest) + element_shift
        state_cov = (
            jnp.dot(
                jnp.dot(element_map, state_cov, precision=highest), element_map.T, precision=highest
            )
            + element_noise
        )
        return ((state_mean, state_cov), (state_mean, jnp.diagonal(state_cov)))

    _, (means, variances) = lax.scan(advance, (entry_mean, entry_cov), (step_map, shift, noise))
    return (means, variances)


def solution(mesh):
    return jax.shard_map(
        per_device,
        mesh=mesh,
        in_specs=(
            P(),
            P(),
            P(("row", "col"), None),
            P(("row", "col"), None, None),
            P(("row", "col"), None, None),
            P(("row", "col"), None, None),
            P(),
            P(),
            P(("row", "col"), None),
        ),
        out_specs=(P(("row", "col"), None), P(("row", "col"), None)),
        check_vma=False,
    )
```

profile of v0, /device:TPU:1, one launch (start us, length us, event | category | flops | bytes accessed | tf_op | source)
XLA Modules:
  0.0 880.2 jit_solution(12494326591133280143)
XLA Ops:
  7.5 6.6 copy.22
  15.6 6.7 bitcast_subtract_fusion.1
  22.3 9.0 %copy.27 = f32[32,256,256]{2,1,0:T(8,128)} copy(f32[32,256,256]{1,2,0:T(8,128)} %bitcast_subtract_fusion.1) | data formatting | bytes 16777216
  31.3 4.6 fusion.76
  36.4 8.2 bitcast_add_fusion
  44.6 176.0 %while.68 = (s32[]{:T(128)}, f32[256,256]{1,0:T(8,128)S(1)}, f32[256]{0:T(256)S(1)}, f32[256,256]{1,0:T(8,128)S(1)}, f32[32,256,256]{2,1,0:T(8,128)}, /*index=5*...) while((s32[]{:T(128)}, f32[256,256]{1,0:T(8,128)S(1)}, f32[256]{0:T(256)S(1)}, ...), condition=%wide.region_1.2_spmd.clone, body=%wide.region_0.1_spmd.clone.sunk | while | flops 604897792 | bytes 3419756 | solution.py:84
  222.1 11.9 %all-gather.3 = f32[8,1,256]{2,1,0:T(1,128)S(1)} all-gather(f32[1,1,256]{2,1,0:T(1,128)S(1)} %bitcast.251), channel_id=3, replica_groups=mesh['row'=16,'col'=8] {'col'}, dimensions={0}, use_global_device_ids=true | all-gather | bytes 9216 | tf_op jit(solution)/shard_map/all_gather | solution.py:11
  234.0 16.3 %all-gather.14.cloned.1.call-done = f32[2048,256]{1,0:T(8,128)} async-done(((f32[256,256]{1,0:T(8,128)}), f32[2048,256]{1,0:T(8,128)}) %all-gather.14.cloned.1.call-update) | async-done | bytes 2097168 | tf_op jit(solution)/shard_map/all_gather | solution.py:11
  250.3 27.4 %all-gather.16.cloned.1.call-done = f32[2048,256]{1,0:T(8,128)} async-done(((f32[256,256]{1,0:T(8,128)}), f32[2048,256]{1,0:T(8,128)}) %all-gather.16.cloned.1.call-update) | async-done | bytes 2097168 | tf_op jit(solution)/shard_map/all_gather | solution.py:11
  277.8 44.5 %while.69 = (s32[]{:T(128)}, f32[256,256]{1,0:T(8,128)S(1)}, f32[256]{0:T(256)S(1)}, f32[256,256]{1,0:T(8,128)S(1)}, s32[]{:T(128)}, /*index=5*/f32[8,256,256]{2...) while((s32[]{:T(128)}, f32[256,256]{1,0:T(8,128)S(1)}, ...), condition=%wide.region_3.4_spmd.clone, body=%wide.region_2.3_spmd.clone.sunk | while | flops 605094912 | bytes 3945090 | solution.py:23
  324.9 59.2 %all-reduce.3.cloned.1.call-done = (f32[1,256,256]{2,1,0:T(8,128)}, f32[1,256,256]{2,1,0:T(8,128)}) async-done(((f32[1,256,256]{2,1,0:T(8,128)}, f32[1,256,256]{2,1,0:T(8,128)}), (f32[1,256,256]{2,1,0:T(8,128)}, f32[1,256,256]{2,1,0:T(8,128)})) %all-reduce.3.cloned.1.call-update) | async-done | bytes 524304 | tf_op jit(solution)/shard_map/psum | solution.py:28
  385.1 14.5 %psum.22 = f32[1,256]{1,0:T(1,128)S(1)} all-reduce(f32[1,256]{1,0:T(1,128)S(1)} %bitcast.257), channel_id=1, replica_groups=mesh['row'=16,'col'=8] {'col'}, use_global_device_ids=true, to_apply=%region_5.6 | all-reduce | flops 256 | bytes 2048 | tf_op jit(solution)/shard_map/psum | solution.py:28
  399.7 19.0 %all-gather.4 = f32[16,1,256]{2,1,0:T(1,128)S(1)} all-gather(f32[1,1,256]{2,1,0:T(1,128)S(1)} %bitcast.258), channel_id=1, replica_groups=mesh['row'=16,'col'=8] {'row'}, dimensions={0}, use_global_device_ids=true | all-gather | bytes 17408 | tf_op jit(solution)/shard_map/all_gather | solution.py:11
  418.7 20.2 %all-gather.10.cloned.1.call-done = f32[16,256,256]{2,1,0:T(8,128)} async-done(((f32[1,256,256]{2,1,0:T(8,128)}), f32[16,256,256]{2,1,0:T(8,128)}) %all-gather.10.cloned.1.call-update) | async-done | bytes 4194320 | tf_op jit(solution)/shard_map/all_gather | solution.py:11
  438.9 53.0 %all-gather.12.cloned.1.call-done = f32[16,256,256]{2,1,0:T(8,128)} async-done(((f32[1,256,256]{2,1,0:T(8,128)}), f32[16,256,256]{2,1,0:T(8,128)}) %all-gather.12.cloned.1.call-update) | async-done | bytes 4194320 | tf_op jit(solution)/shard_map/all_gather | solution.py:11
  491.9 88.8 %while.70 = (s32[]{:T(128)}, f32[256,256]{1,0:T(8,128)S(1)}, f32[256]{0:T(256)S(1)}, f32[256,256]{1,0:T(8,128)S(1)}, s32[]{:T(128)}, /*index=5*/f32[16,256,256]{...) while((s32[]{:T(128)}, f32[256,256]{1,0:T(8,128)S(1)}, ...), condition=%wide.region_8.9_spmd.clone, body=%wide.region_7.8_spmd.clone.sunk | while | flops 605094912 | bytes 3945090 | solution.py:23
  583.0 290.6 %while.67 = (s32[]{:T(128)}, f32[256]{0:T(256)S(1)}, f32[256,256]{1,0:T(8,128)S(1)}, f32[32,256]{1,0:T(8,128)}, f32[32,256]{1,0:T(8,128)}, /*index=5*/f32[32,256...) while((s32[]{:T(128)}, f32[256]{0:T(256)S(1)}, ...), condition=%wide.region_10.11_spmd, body=%wide.region_9.10_spmd.sunk | while | flops 403506432 | bytes 2115697 | solution.py:110
  585.9 2.3 gather_fusion
  594.9 2.3 gather_fusion
  613.1 2.3 gather_fusion
  622.2 2.3 gather_fusion
  631.3 2.3 gather_fusion
  649.4 2.3 gather_fusion
  658.5 2.3 gather_fusion
  667.6 2.3 gather_fusion
  676.7 2.3 gather_fusion
  694.8 2.3 gather_fusion
  703.9 2.3 gather_fusion
  713.0 2.3 gather_fusion
  731.2 2.3 gather_fusion
  740.3 2.3 gather_fusion
  749.3 2.3 gather_fusion
  (793 shorter events, 568.8 us)
Async XLA Ops:
  7.2 28.7 %copy-start = (f32[32,64]{1,0:T(8,128)S(1)}, f32[32,64]{1,0:T(8,128)}, u32[]{:S(2)}) copy-start(f32[32,64]{1,0:T(8,128)} %param.25) | copy-start | bytes 24580
  7.2 243.2 %all-gather.14.cloned.1.call-start = ((), (), s32[]{:S(2)}) async-start(), calls=%async_computation.2 | async-start | bytes 2359296 | tf_op jit(solution)/shard_map/all_gather | solution.py:11
  7.2 15.1 %copy-start.1 = (f32[256,256]{1,0:T(8,128)}, f32[256,256]{1,0:T(8,128)S(1)}, u32[]{:S(2)}) copy-start(f32[256,256]{1,0:T(8,128)S(1)} %fusion.85) | copy-start | bytes 786436
  7.4 6.7 copy-start.12
  7.4 6.8 copy-start.10
  7.4 8.2 copy-start.7
  7.5 8.2 copy-start.13
  22.3 9.0 %copy-start.16 = (f32[64]{0:T(128)S(1)}, f32[64]{0:T(128)}, u32[]{:S(2)}) copy-start(f32[64]{0:T(128)} %param.24) | copy-start | bytes 772
  31.3 5.1 copy-start.11
  36.4 8.2 copy-start.5
  44.6 233.2 %copy-start.6 = (f32[256,256]{1,0:T(8,128)S(1)}, f32[256,256]{1,0:T(8,128)}, u32[]{:S(2)}) copy-start(f32[256,256]{1,0:T(8,128)} %copy-done.1) | copy-start | bytes 786436
  220.6 0.7 copy-start.3
  220.6 0.8 copy-start.8
  221.3 56.4 %all-gather.16.cloned.1.call-start = ((), (), s32[]{:S(2)}) async-start(), calls=%async_computation.3 | async-start | bytes 2359296 | tf_op jit(solution)/shard_map/all_gather | solution.py:11
  222.1 162.1 %all-reduce.3.cloned.1.call-start = ((), (), s32[]{:S(2)}) async-start(), calls=%async_computation.4 | async-start | bytes 1048576 | tf_op jit(solution)/shard_map/psum | solution.py:28
  277.8 44.5 %copy-start.4 = (f32[256,256]{1,0:T(8,128)S(1)}, f32[256,256]{1,0:T(8,128)}, u32[]{:S(2)}) copy-start(f32[256,256]{1,0:T(8,128)} %copy-done.3) | copy-start | bytes 786436
  277.8 44.9 %copy-start.9 = (f32[256,256]{1,0:T(8,128)S(1)}, f32[256,256]{1,0:T(8,128)}, u32[]{:S(2)}) copy-start(f32[256,256]{1,0:T(8,128)} %copy-done.8) | copy-start | bytes 786436
  277.8 214.2 %copy-start.2 = (f32[256,256]{1,0:T(8,128)S(1)}, f32[256,256]{1,0:T(8,128)}, u32[]{:S(2)}) copy-start(f32[256,256]{1,0:T(8,128)} %copy-done.1) | copy-start | bytes 786436
  324.9 114.0 %all-gather.10.cloned.1.call-start = ((), (), s32[]{:S(2)}) async-start(), calls=%async_computation | async-start | bytes 4456448 | tf_op jit(solution)/shard_map/all_gather | solution.py:11
  384.2 107.8 %all-gather.12.cloned.1.call-start = ((), (), s32[]{:S(2)}) async-start(), calls=%async_computation.1 | async-start | bytes 4456448 | tf_op jit(solution)/shard_map/all_gather | solution.py:11
  491.9 89.9 %copy-start.14 = (f32[256]{0:T(256)S(1)}, f32[256]{0:T(256)}, u32[]{:S(2)}) copy-start(f32[256]{0:T(256)} %param.18) | copy-start | bytes 3076
  491.9 90.3 %copy-start.15 = (f32[256]{0:T(256)S(1)}, f32[256]{0:T(256)}, u32[]{:S(2)}) copy-start(f32[256]{0:T(256)} %param.17) | copy-start | bytes 3076
Sparse Core Ops, SparseCore 0:
  221.4 28.8 all-gather.13
  252.1 25.6 all-gather.15
  325.0 59.0 all-reduce.2
  386.1 52.7 all-gather.9
  440.9 51.0 all-gather.11
where the time goes:
time: 892 us; the launch traced here: 880 us
  matrix products  454 us (51%)
  local copies, waits for them, and re-layouts  182 us (20%)
  waiting for transfers between devices  177 us (20%)
  blocking collectives  45.5 us (5%)
  between operations  14.1 us (2%)
    all_gather x4, waiting for transfers between devices, entering(): everything = jax.tree.map(lambda part: lax.all_gather(part, axis), shard)  117 us
    dynamic_update_slice x64, local copies, waits for them, and re-layouts, per_device(): lax.scan(advance, (entry_mean, entry_cov), (step_map, shift, noise))  84.2 us
    dot_general x58, matrix products, combine(): jnp.matmul(moved, jnp.swapaxes(later_map, -1, -2), precision=highest)  83.6 us
    dot_general x58, matrix products, combine(): joined_map = jnp.matmul(later_map, earlier_map, precision=highest)  76.2 us
    dot_general x58, matrix products, combine(): moved = jnp.matmul(later_map, earlier_noise, precision=highest)  75.6 us
    gather x32, local copies, waits for them, and re-layouts, advance(): return ((state_mean, state_cov), (state_mean, jnp.diagonal(state_cov)))  75 us
    dot_general x58, matrix products, combine(): jnp.einsum('...ij,...j->...i', later_map, earlier_shift, precision=highest)  69.1 us
    psum x1, waiting for transfers between devices, broadcast(): return lax.psum(block, axis)  59.2 us
  transfers between devices with their start and end apart: 5, of which 5 were waited for; matrix products, arithmetic and copies ran while one was open for 0% of the time, Pallas kernels for 0%

commit v1 on v0

v1 whole, which is shorter than its diff:
```python
import functools

import jax
import jax.numpy as jnp
from jax import lax
from jax.experimental import pallas as pl
from jax.experimental.pallas import tpu as pltpu
from jax.sharding import PartitionSpec as P

highest = lax.Precision.HIGHEST
f32 = jnp.float32
bf16 = jnp.bfloat16
PAD = 16
SPB = 4


def dot_nn(a, b):
    return lax.dot_general(a, b, (((1,), (0,)), ((), ())), preferred_element_type=f32)


def dot_nt(a, b):
    return lax.dot_general(a, b, (((1,), (1,)), ((), ())), preferred_element_type=f32)


def split(x):
    hi = x.astype(bf16)
    return hi, (x - hi.astype(f32)).astype(bf16)


def eye(n):
    row = lax.broadcasted_iota(jnp.int32, (n, n), 0)
    col = lax.broadcasted_iota(jnp.int32, (n, n), 1)
    return row == col


def local_kernel(steps, decay_ref, observed_ref, var_ref, coupling_ref, map_ref, gain_ref,
                 factor_ref, hi_ref, lo_ref, diag_ref, shift_ref, total_ref,
                 state, e_hi, e_lo, noise, shift):
    i = pl.program_id(0)
    s = decay_ref.shape[1]
    put = lax.rem(i, 2)
    get = 1 - put

    @pl.when(i <= 1)
    def _():
        unit = jnp.where(eye(s), 1.0, 0.0).astype(f32)
        state[...] = jnp.concatenate([unit, jnp.zeros((s + PAD, s), f32)], axis=0)

    factor = factor_ref[...]
    block = jnp.minimum(i, pl.num_programs(0) - 2)
    for j in range(steps):
        t = block * steps + j
        decay = decay_ref[pl.ds(t, 1), :]
        obs_map = map_ref[j]
        gain = gain_ref[j]
        coupling = coupling_ref[j]
        gain_t = gain.T
        obs_f = (obs_map.astype(f32) * decay + dot_nn(obs_map, coupling)).astype(bf16)
        obs_g = dot_nn(obs_map, factor).astype(bf16)
        e = coupling.astype(f32) - dot_nn(gain_t, obs_f)
        hi, lo = split(e)
        e_hi[put, j] = hi
        e_lo[put, j] = lo
        shaped = (factor.astype(f32) - dot_nn(gain_t, obs_g)).astype(bf16)
        weighted = (gain.astype(f32) * var_ref[...]).astype(bf16)
        noise[put, j] = dot_nt(shaped, shaped) + dot_nn(gain_t, weighted)
        z_hi, z_lo = split(jnp.broadcast_to(observed_ref[pl.ds(t, 1), :], (PAD, gain.shape[0])))
        shift[put, j] = dot_nn(z_hi, gain) + dot_nn(z_lo, gain)

    block = jnp.maximum(i - 1, 0)
    diagonal = eye(s)
    x = state[...]
    for j in range(steps):
        t = block * steps + j
        decay = decay_ref[pl.ds(t, 1), :]
        decay_t = jnp.broadcast_to(decay, (8, s)).T[:, 0:1]
        eh, el = e_hi[get, j], e_lo[get, j]
        x_hi, x_lo = split(x)
        y = x * decay + (dot_nt(x_hi, eh) + (dot_nt(x_lo, eh) + dot_nt(x_hi, el)))
        maps, v, b = y[:s], y[s:2 * s], y[2 * s:]
        m_hi, m_lo = split(maps)
        hi_ref[j] = m_hi
        lo_ref[j] = m_lo
        v_hi, v_lo = split(v)
        n = v * decay_t + noise[get, j] + (dot_nn(eh, v_hi) + (dot_nn(eh, v_lo) + dot_nn(el, v_hi)))
        b = b + shift[get, j]
        diag_ref[pl.ds(t, 1), :] = jnp.sum(jnp.where(diagonal, n, 0.0), axis=0, keepdims=True)
        shift_ref[pl.ds(t, 1), :] = b[0:1]
        x = jnp.concatenate([maps, n, b], axis=0)
    state[...] = x

    @pl.when(i == pl.num_programs(0) - 1)
    def _():
        total_ref[...] = x


def local_prefix(decay, coupling, obs_map, gain, factor, obs_var, observed):
    count, s = decay.shape
    m = obs_map.shape[1]
    steps = SPB
    blocks = count // steps
    ahead = lambda i: (jnp.minimum(i, blocks - 1), 0, 0)
    behind = lambda i: (jnp.maximum(i - 1, 0), 0, 0)
    whole = lambda i: (0, 0)
    return pl.pallas_call(
        functools.partial(local_kernel, steps),
        grid=(blocks + 1,),
        in_specs=[
            pl.BlockSpec((count, s), whole),
            pl.BlockSpec((count, m), whole),
            pl.BlockSpec((m, 1), whole),
            pl.BlockSpec((steps, s, s), ahead),
            pl.BlockSpec((steps, m, s), ahead),
            pl.BlockSpec((steps, m, s), ahead),
            pl.BlockSpec((s, s), whole),
        ],
        out_specs=[
            pl.BlockSpec((steps, s, s), behind),
            pl.BlockSpec((steps, s, s), behind),
            pl.BlockSpec((count, s), whole),
            pl.BlockSpec((count, s), whole),
            pl.BlockSpec((2 * s + PAD, s), whole),
        ],
        out_shape=[
            jax.ShapeDtypeStruct((count, s, s), bf16),
            jax.ShapeDtypeStruct((count, s, s), bf16),
            jax.ShapeDtypeStruct((count, s), f32),
            jax.ShapeDtypeStruct((count, s), f32),
            jax.ShapeDtypeStruct((2 * s + PAD, s), f32),
        ],
        scratch_shapes=[
            pltpu.VMEM((2 * s + PAD, s), f32),
            pltpu.VMEM((2, steps, s, s), bf16),
            pltpu.VMEM((2, steps, s, s), bf16),
            pltpu.VMEM((2, steps, s, s), f32),
            pltpu.VMEM((2, steps, PAD, s), f32),
        ],
        name="local_prefix",
    )(decay, observed, obs_var[:, None], coupling, obs_map, gain, factor)


def output_kernel(steps, entry_ref, hi_ref, lo_ref, diag_ref, shift_ref, mean_ref, var_ref, left):
    i = pl.program_id(0)
    s = hi_ref.shape[2]
    rows = s + PAD

    @pl.when(i == 0)
    def _():
        hi, lo = split(entry_ref[...])
        left[:rows] = hi
        left[rows:] = lo

    for j in range(steps):
        t = i * steps + j
        hi, lo = hi_ref[j], lo_ref[j]
        both = dot_nn(left[...], hi)
        r = both[:rows] + (both[rows:] + dot_nn(left[:rows], lo))
        maps = hi.astype(f32) + lo.astype(f32)
        var_ref[pl.ds(t, 1), :] = (
            jnp.sum(r[:s] * maps, axis=0, keepdims=True) + diag_ref[pl.ds(t, 1), :]
        )
        mean_ref[pl.ds(t, 1), :] = r[s:s + 1] + shift_ref[pl.ds(t, 1), :]


def outputs(entry, hi, lo, diag, shift):
    count, s = diag.shape
    steps = SPB
    whole = lambda i: (0, 0)
    return pl.pallas_call(
        functools.partial(output_kernel, steps),
        grid=(count // steps,),
        in_specs=[
            pl.BlockSpec((s + PAD, s), whole),
            pl.BlockSpec((steps, s, s), lambda i: (i, 0, 0)),
            pl.BlockSpec((steps, s, s), lambda i: (i, 0, 0)),
            pl.BlockSpec((count, s), whole),
            pl.BlockSpec((count, s), whole),
        ],
        out_specs=[pl.BlockSpec((count, s), whole), pl.BlockSpec((count, s), whole)],
        out_shape=[jax.ShapeDtypeStruct((count, s), f32)] * 2,
        scratch_shapes=[pltpu.VMEM((2 * (s + PAD), s), bf16)],
        name="outputs",
    )(entry, hi, lo, diag, shift)


def entering(shard, axis, combine, identity):
    size, place = (lax.axis_size(axis), lax.axis_index(axis))
    everything = jax.tree.map(lambda part: lax.all_gather(part, axis), shard)
    start = jax.tree.map(
        lambda part, zero: jnp.broadcast_to(jnp.asarray(zero, part.dtype), part.shape),
        shard,
        identity,
    )

    def hop(k, before):
        reached = k < place
        new = combine(before, jax.tree.map(lambda part: part[k], everything))
        return jax.tree.map(lambda a, b: jnp.where(reached, a, b), new, before)

    return lax.fori_loop(0, size, hop, start)


def broadcast(block, axis, holder):
    block = jnp.where(lax.axis_index(axis) == holder, block, jnp.zeros_like(block))
    return lax.psum(block, axis)


def combine(earlier, later):
    earlier_map, earlier_shift, earlier_noise = earlier
    later_map, later_shift, later_noise = later
    joined_map = jnp.matmul(later_map, earlier_map, precision=highest)
    joined_shift = jnp.einsum("ij,j->i", later_map, earlier_shift, precision=highest) + later_shift
    moved = jnp.matmul(later_map, earlier_noise, precision=highest)
    joined_noise = jnp.matmul(moved, later_map.T, precision=highest) + later_noise
    return (joined_map, joined_shift, joined_noise)


def entry_of(total, init_mean, init_var):
    s = init_mean.shape[0]
    neutral = (jnp.eye(s, dtype=f32), jnp.zeros((s,), f32), jnp.zeros((s, s), f32))
    element = (total[:s].T, total[2 * s], total[s:2 * s])
    inner = entering(element, "col", combine, neutral)
    row_whole = combine(inner, element)
    row_total = tuple(broadcast(part, "col", lax.axis_size("col") - 1) for part in row_whole)
    outer = entering(row_total, "row", combine, neutral)
    carry_map, carry_shift, carry_noise = combine(outer, inner)
    mean = jnp.dot(carry_map, init_mean, precision=highest) + carry_shift
    cov = jnp.dot(carry_map * init_var[None, :], carry_map.T, precision=highest) + carry_noise
    return jnp.concatenate([cov, jnp.broadcast_to(mean, (PAD, s))], axis=0)


def per_device(
    init_mean, init_var, decay, coupling, obs_map, gain, noise_factor, obs_var, observed
):
    hi, lo, diag, shift, total = local_prefix(
        decay, coupling, obs_map, gain, noise_factor, obs_var, observed
    )
    entry = entry_of(total, init_mean, init_var)
    means, variances = outputs(entry, hi, lo, diag, shift)
    return (means, variances)


def solution(mesh):
    return jax.shard_map(
        per_device,
        mesh=mesh,
        in_specs=(
            P(),
            P(),
            P(("row", "col"), None),
            P(("row", "col"), None, None),
            P(("row", "col"), None, None),
            P(("row", "col"), None, None),
            P(),
            P(),
            P(("row", "col"), None),
        ),
        out_specs=(P(("row", "col"), None), P(("row", "col"), None)),
        check_vma=False,
    )
```

time: 892 us -> 411 us (0.46); the launches traced: 880 us -> 408 us
  matrix products: 454 us -> 111 us
  local copies, waits for them, and re-layouts: 182 us -> 6.64 us
  Pallas kernels: 0 us -> 51.5 us
    dot_general x219 -> x54, matrix products: 302 us -> 59.8 us  [the longest x26 36.7 us: combine(): jnp.matmul(moved, later_map.T, precision=highest) + later_noise]
    dynamic_update_slice x64 -> x0, local copies, waits for them, and re-layouts: 84.2 us -> none  [per_device(): lax.scan(advance, (entry_mean, entry_cov), (step_map, shift, noise))]
    gather x32 -> x0, local copies, waits for them, and re-layouts: 75 us -> none  [advance(): return ((state_mean, state_cov), (state_mean, jnp.diagonal(state_cov)))]
    pallas_call x0 -> x2, Pallas kernels: none -> 51.5 us  [the longest x1 42.6 us: local_prefix(): pl.pallas_call(functools.partial(local_kernel, steps), grid=(blocks + 1,)...]
    dot_general x58 -> x26, matrix products: 75.6 us -> 25.5 us  [combine(): moved = jnp.matmul(later_map, earlier_noise, precision=highest)]
    dot_general x58 -> x26, matrix products: 76.2 us -> 26.2 us  [combine(): joined_map = jnp.matmul(later_map, earlier_map, precision=highest)]
    unnamed x38 -> x10, local copies, waits for them, and re-layouts: 16.4 us -> 1.96 us
  transfers between devices with their start and end apart: 5 -> 5, of which waited for: 5 -> 5; matrix products, arithmetic and copies ran while one was open for 0% -> 1% of each run, Pallas kernels for 0% -> 0%
where the time goes in v1:
time: 411 us; the launch traced here: 408 us
  waiting for transfers between devices  175 us (43%)
  matrix products  111 us (27%)
  Pallas kernels  51.5 us (13%)
  blocking collectives  45.3 us (11%)
  between operations  14 us (3%)
  local copies, waits for them, and re-layouts  6.64 us (2%)
    all_gather x4, waiting for transfers between devices, entering(): everything = jax.tree.map(lambda part: lax.all_gather(part, axis), shard)  114 us
    psum x1, waiting for transfers between devices, broadcast(): return lax.psum(block, axis)  59.2 us
    pallas_call x1, Pallas kernels, local_prefix(): pl.pallas_call(functools.partial(local_kernel, steps), grid=(blocks + 1,)...  42.6 us
    dot_general x26, matrix products, combine(): jnp.matmul(moved, later_map.T, precision=highest) + later_noise  36.7 us
    all_gather x2, blocking collectives, entering(): everything = jax.tree.map(lambda part: lax.all_gather(part, axis), shard)  30.8 us
    dot_general x26, matrix products, combine(): joined_map = jnp.matmul(later_map, earlier_map, precision=highest)  26.2 us
    dot_general x26, matrix products, combine(): moved = jnp.matmul(later_map, earlier_noise, precision=highest)  25.5 us
    dot_general x26, matrix products, combine(): jnp.einsum('ij,j->i', later_map, earlier_shift, precision=highest)  22.3 us
  transfers between devices with their start and end apart: 5, of which 5 were waited for; matrix products, arithmetic and copies ran while one was open for 1% of the time, Pallas kernels for 0%

profile of v1, /device:TPU:1, one launch (start us, length us, event | category | flops | bytes accessed | tf_op | source)
XLA Modules:
  0.0 408.1 jit_solution(15781561207983080239)
XLA Ops:
  8.6 42.6 %local_prefix.1 = (bf16[32,256,256]{2,1,0:T(8,128)(2,1)}, bf16[32,256,256]{2,1,0:T(8,128)(2,1)}, f32[32,256]{1,0:T(8,128)}, f32[32,256]{1,0:T(8,128)}, f32[528,256]{1,0:T(8,128)}) custom-call(f32[32,256]{1,0:T(8,128)} %decay_ref.1, f32[32,64]{1,0:T(8,128)} %observed_ref.1, f32[64,1]{1,0:T(8,128)} %copy.13.var_ref, bf16[32,256,256]{2,1,0:T(8,128)(2,1)} %coupling_ref.1, ...), custom_call_target="tpu_custom_call" | custom-call | tf_op jit(solution)/shard_map/local_prefix/pallas_call | solution.py:105
  51.2 1.9 fusion.52
  54.7 11.9 %all-gather.2 = f32[8,1,256]{2,1,0:T(1,128)S(1)} all-gather(f32[1,1,256]{2,1,0:T(1,128)S(1)} %get-tuple-element.405), channel_id=1, replica_groups=mesh['row'=16,'col'=8] {'col'}, dimensions={0}, use_global_device_ids=true | all-gather | bytes 9216 | tf_op jit(solution)/shard_map/all_gather | solution.py:188
  66.5 15.6 %all-gather.13.cloned.1.call-done = f32[2048,256]{0,1:T(8,128)} async-done(((f32[256,256]{0,1:T(8,128)}), f32[2048,256]{0,1:T(8,128)}) %all-gather.13.cloned.1.call-update) | async-done | bytes 2097168 | tf_op jit(solution)/shard_map/all_gather | solution.py:188
  82.1 1.9 copy.15
  84.0 25.4 %all-gather.15.cloned.1.call-done = f32[2048,256]{1,0:T(8,128)} async-done(((f32[256,256]{1,0:T(8,128)}), f32[2048,256]{1,0:T(8,128)}) %all-gather.15.cloned.1.call-update) | async-done | bytes 2097168 | tf_op jit(solution)/shard_map/all_gather | solution.py:188
  109.4 21.1 %while.36 = (s32[]{:T(128)}, f32[256,256]{1,0:T(8,128)S(1)}, f32[256]{0:T(256)S(1)}, f32[256,256]{1,0:T(8,128)S(1)}, s32[]{:T(128)}, /*index=5*/f32[8,256,256]{2...) while((s32[]{:T(128)}, f32[256,256]{1,0:T(8,128)S(1)}, ...), condition=%wide.region_1.2_spmd.clone, body=%wide.region_0.1_spmd.clone.sunk | while | flops 605094912 | bytes 3944596 | solution.py:200
  113.3 1.4 fusion.110
  121.2 1.4 fusion.110
  133.6 59.2 %all-reduce.3.cloned.1.call-done = (f32[1,256,256]{2,1,0:T(8,128)}, f32[1,256,256]{2,1,0:T(8,128)}) async-done(((f32[1,256,256]{2,1,0:T(8,128)}, f32[1,256,256]{2,1,0:T(8,128)}), (f32[1,256,256]{2,1,0:T(8,128)}, f32[1,256,256]{2,1,0:T(8,128)})) %all-reduce.3.cloned.1.call-update) | async-done | bytes 524304 | tf_op jit(solution)/shard_map/psum | solution.py:205
  193.8 14.5 %psum.22 = f32[1,256]{1,0:T(1,128)S(1)} all-reduce(f32[1,256]{1,0:T(1,128)S(1)} %bitcast.137), channel_id=1, replica_groups=mesh['row'=16,'col'=8] {'col'}, use_global_device_ids=true, to_apply=%region_3.4 | all-reduce | flops 256 | bytes 2048 | tf_op jit(solution)/shard_map/psum | solution.py:205
  208.3 18.9 %all-gather.3 = f32[16,1,256]{2,1,0:T(1,128)S(1)} all-gather(f32[1,1,256]{2,1,0:T(1,128)S(1)} %bitcast.138), channel_id=1, replica_groups=mesh['row'=16,'col'=8] {'row'}, dimensions={0}, use_global_device_ids=true | all-gather | bytes 17408 | tf_op jit(solution)/shard_map/all_gather | solution.py:188
  227.2 20.4 %all-gather.9.cloned.1.call-done = f32[16,256,256]{2,1,0:T(8,128)} async-done(((f32[1,256,256]{2,1,0:T(8,128)}), f32[16,256,256]{2,1,0:T(8,128)}) %all-gather.9.cloned.1.call-update) | async-done | bytes 4194320 | tf_op jit(solution)/shard_map/all_gather | solution.py:188
  247.5 53.1 %all-gather.11.cloned.1.call-done = f32[16,256,256]{2,1,0:T(8,128)} async-done(((f32[1,256,256]{2,1,0:T(8,128)}), f32[16,256,256]{2,1,0:T(8,128)}) %all-gather.11.cloned.1.call-update) | async-done | bytes 4194320 | tf_op jit(solution)/shard_map/all_gather | solution.py:188
  300.6 89.0 %while.37 = (s32[]{:T(128)}, f32[256,256]{1,0:T(8,128)S(1)}, f32[256]{0:T(256)S(1)}, f32[256,256]{1,0:T(8,128)S(1)}, s32[]{:T(128)}, /*index=5*/f32[16,256,256]{...) while((s32[]{:T(128)}, f32[256,256]{1,0:T(8,128)S(1)}, ...), condition=%wide.region_6.7_spmd.clone, body=%wide.region_5.6_spmd.clone.sunk | while | flops 605094912 | bytes 3944596 | solution.py:200
  304.7 1.5 fusion.121
  310.2 1.5 fusion.121
  315.8 1.5 fusion.121
  321.4 1.5 fusion.121
  326.9 1.5 fusion.121
  332.5 1.5 fusion.121
  338.1 1.5 fusion.121
  343.6 1.5 fusion.121
  349.2 1.5 fusion.121
  354.7 1.5 fusion.121
  360.3 1.5 fusion.121
  365.9 1.5 fusion.121
  371.4 1.5 fusion.121
  377.0 1.5 fusion.121
  382.6 1.5 fusion.121
  388.1 1.5 fusion.121
  392.7 8.9 %outputs.1 = (f32[32,256]{1,0:T(8,128)}, f32[32,256]{1,0:T(8,128)}) custom-call(f32[272,256]{1,0:T(8,128)} %pad_maximum_fusion.entry_ref, bf16[32,256,256]{2,1,0:T(8,128)(2,1)} %get-tuple-element.296.hi_ref, bf16[32,256,256]{2,1,0:T(8,128)(2,1)} %get-tuple-element.297.lo_ref, f32[32,256]{1,0:T(8,128)} %get-tuple-element.298.diag_ref, ...), custom_call_target="tpu_custom_call" | custom-call | tf_op jit(solution)/shard_map/outputs/pallas_call | solution.py:169
  (214 shorter events, 91.5 us)
Async XLA Ops:
  7.2 383.6 %copy-start = (f32[256]{0:T(256)S(1)}, f32[256]{0:T(256)}, u32[]{:S(2)}) copy-start(f32[256]{0:T(256)} %param.13) | copy-start | bytes 3076
  7.2 74.9 %all-gather.13.cloned.1.call-start = ((), (), s32[]{:S(2)}) async-start(), calls=%async_computation.2 | async-start | bytes 2359296 | tf_op jit(solution)/shard_map/all_gather | solution.py:188
  53.1 56.4 %all-gather.15.cloned.1.call-start = ((), (), s32[]{:S(2)}) async-start(), calls=%async_computation.3 | async-start | bytes 2359296 | tf_op jit(solution)/shard_map/all_gather | solution.py:188
  53.8 139.0 %all-reduce.3.cloned.1.call-start = ((), (), s32[]{:S(2)}) async-start(), calls=%async_computation.4 | async-start | bytes 1048576 | tf_op jit(solution)/shard_map/psum | solution.py:205
  109.4 21.1 %copy-start.1 = (f32[528,256]{1,0:T(8,128)S(1)}, f32[528,256]{1,0:T(8,128)}, u32[]{:S(2)}) copy-start(f32[528,256]{1,0:T(8,128)} %get-tuple-element.289) | copy-start | bytes 1622020
  133.6 113.9 %all-gather.9.cloned.1.call-start = ((), (), s32[]{:S(2)}) async-start(), calls=%async_computation | async-start | bytes 4456448 | tf_op jit(solution)/shard_map/all_gather | solution.py:188
  192.9 107.7 %all-gather.11.cloned.1.call-start = ((), (), s32[]{:S(2)}) async-start(), calls=%async_computation.1 | async-start | bytes 4456448 | tf_op jit(solution)/shard_map/all_gather | solution.py:188
  300.6 90.4 %copy-start.2 = (f32[256]{0:T(256)S(1)}, f32[256]{0:T(256)}, u32[]{:S(2)}) copy-start(f32[256]{0:T(256)} %param.14) | copy-start | bytes 3076
Sparse Core Ops, SparseCore 0:
  53.2 28.8 all-gather.12
  83.8 25.5 all-gather.14
  133.7 59.0 all-reduce.2
  194.9 52.6 all-gather.8
  249.5 51.0 all-gather.10

commit v2 on v1

--- a/solution.py
+++ b/solution.py
@@ -7,7 +7,6 @@
 from jax.experimental.pallas import tpu as pltpu
 from jax.sharding import PartitionSpec as P
 
-highest = lax.Precision.HIGHEST
 f32 = jnp.float32
 bf16 = jnp.bfloat16
 PAD = 16
@@ -183,50 +182,177 @@
     )(entry, hi, lo, diag, shift)
 
 
-def entering(shard, axis, combine, identity):
-    size, place = (lax.axis_size(axis), lax.axis_index(axis))
-    everything = jax.tree.map(lambda part: lax.all_gather(part, axis), shard)
-    start = jax.tree.map(
-        lambda part, zero: jnp.broadcast_to(jnp.asarray(zero, part.dtype), part.shape),
-        shard,
-        identity,
-    )
-
-    def hop(k, before):
-        reached = k < place
-        new = combine(before, jax.tree.map(lambda part: part[k], everything))
-        return jax.tree.map(lambda a, b: jnp.where(reached, a, b), new, before)
-
-    return lax.fori_loop(0, size, hop, start)
-
-
-def broadcast(block, axis, holder):
-    block = jnp.where(lax.axis_index(axis) == holder, block, jnp.zeros_like(block))
-    return lax.psum(block, axis)
-
-
-def combine(earlier, later):
-    earlier_map, earlier_shift, earlier_noise = earlier
-    later_map, later_shift, later_noise = later
-    joined_map = jnp.matmul(later_map, earlier_map, precision=highest)
-    joined_shift = jnp.einsum("ij,j->i", later_map, earlier_shift, precision=highest) + later_shift
-    moved = jnp.matmul(later_map, earlier_noise, precision=highest)
-    joined_noise = jnp.matmul(moved, later_map.T, precision=highest) + later_noise
-    return (joined_map, joined_shift, joined_noise)
+MESH_ID = pl.DeviceIdType.MESH
+
+
+def join(first, later, lead):
+    s = later.shape[1]
+    t_hi, t_lo = split(later[:s])
+    x_hi, x_lo = split(first)
+    y = dot_nn(x_hi, t_hi) + (dot_nn(x_lo, t_hi) + dot_nn(x_hi, t_lo))
+    v_hi, v_lo = split(y[lead:lead + s])
+    u_hi, u_lo = t_hi.T, t_lo.T
+    n = dot_nn(u_hi, v_hi) + (dot_nn(u_hi, v_lo) + dot_nn(u_lo, v_hi)) + later[s:2 * s]
+    b = y[lead + s:] + later[2 * s:]
+    parts = [y[:lead], n, b] if lead else [n, b]
+    return jnp.concatenate(parts, axis=0)
+
+
+def scan_kernel(total_ref, mean_ref, var_ref, entry_ref, all_x, all_z, all_y, before_x, before_z,
+                chain, pair, state, send_sem, recv_sem, pair_sem, state_sem):
+    row, col = lax.axis_index("row"), lax.axis_index("col")
+    y, z = row // 4, lax.rem(row, 4)
+    x, core = col // 2, lax.rem(col, 2)
+    s = total_ref.shape[1]
+    half = total_ref.shape[0] // 2
+    upper, lower = pl.ds(0, half), pl.ds(half, half)
+
+    def step(p, by):
+        return lax.rem(p + by, 4)
+
+    def along_x(by):
+        return (row, step(x, by) * 2 + core)
+
+    def along_z(by):
+        return (y * 4 + step(z, by), col)
+
+    def along_y(by):
+        return (step(y, by) * 4 + z, col)
+
+    partner = (row, x * 2 + 1 - core)
+    barrier = pltpu.get_barrier_semaphore()
+    pl.semaphore_signal(barrier, inc=1, device_id=partner, device_id_type=MESH_ID)
+
+    @pl.when(core == 0)
+    def _():
+        for along in (along_x, along_z, along_y):
+            for by in (1, 3):
+                pl.semaphore_signal(barrier, inc=1, device_id=along(by), device_id_type=MESH_ID)
+        pl.semaphore_wait(barrier, 7)
+
+    @pl.when(core == 1)
+    def _():
+        pl.semaphore_wait(barrier, 1)
+
+    def to_first():
+        return pltpu.make_async_remote_copy(
+            src_ref=total_ref, dst_ref=pair, send_sem=pair_sem.at[0], recv_sem=pair_sem.at[1],
+            device_id=partner, device_id_type=MESH_ID)
+
+    def to_second():
+        return pltpu.make_async_remote_copy(
+            src_ref=state, dst_ref=state, send_sem=state_sem.at[0], recv_sem=state_sem.at[1],
+            device_id=partner, device_id_type=MESH_ID)
+
+    def copy(level, hold, place, rows, k, target):
+        return pltpu.make_async_remote_copy(
+            src_ref=hold.at[place, rows], dst_ref=hold.at[place, rows],
+            send_sem=send_sem.at[level, k], recv_sem=recv_sem.at[level, k],
+            device_id=target, device_id_type=MESH_ID)
+
+    def start(level, hold, p, along):
+        right, left = along(1), along(3)
+        copy(level, hold, p, upper, 0, right).start()
+        copy(level, hold, p, lower, 2, left).start()
+        copy(level, hold, p, lower, 1, right).start()
+        copy(level, hold, p, upper, 3, left).start()
+
+    def finish(level, hold, p, along):
+        right, left = along(1), along(3)
+        before, after, across = step(p, 3), step(p, 1), step(p, 2)
+        copy(level, hold, before, upper, 0, right).wait_recv()
+        copy(level, hold, before, upper, 4, right).start()
+        copy(level, hold, after, lower, 2, left).wait_recv()
+        copy(level, hold, after, lower, 5, left).start()
+        copy(level, hold, before, lower, 1, right).wait_recv()
+        copy(level, hold, after, upper, 3, left).wait_recv()
+        copy(level, hold, across, upper, 4, right).wait_recv()
+        copy(level, hold, across, lower, 5, left).wait_recv()
+
+    def drain(level, hold, p, along):
+        right, left = along(1), along(3)
+        copy(level, hold, p, upper, 0, right).wait_send()
+        copy(level, hold, p, lower, 1, right).wait_send()
+        copy(level, hold, p, lower, 2, left).wait_send()
+        copy(level, hold, p, upper, 3, left).wait_send()
+        copy(level, hold, step(p, 3), upper, 4, right).wait_send()
+        copy(level, hold, step(p, 1), lower, 5, left).wait_send()
+
+    def reduce(hold):
+        first = join(hold[0], hold[1], s)
+        last = join(hold[2], hold[3], s)
+        return first, join(first, last, s)
+
+    def prefixes(hold, before, first):
+        unit = jnp.where(eye(s), 1.0, 0.0).astype(f32)
+        before[0] = jnp.concatenate([unit, jnp.zeros((s + PAD, s), f32)], axis=0)
+        before[1] = hold[0]
+        before[2] = first
+        before[3] = join(first, hold[2], s)
+
+    @pl.when(core == 1)
+    def _():
+        to_first().start()
+        to_first().wait_send()
+        to_second().wait_recv()
+        entry_ref[...] = state[...]
+
+    @pl.when(core == 0)
+    def _():
+        to_first().wait_recv()
+        all_x[x] = join(total_ref[...], pair[...], s)
+        start(0, all_x, x, along_x)
+        finish(0, all_x, x, along_x)
+        first, whole = reduce(all_x)
+        all_z[z] = whole
+        start(1, all_z, z, along_z)
+        prefixes(all_x, before_x, first)
+        finish(1, all_z, z, along_z)
+        first, whole = reduce(all_z)
+        all_y[y] = whole
+        start(2, all_y, y, along_y)
+        prefixes(all_z, before_z, first)
+        here = join(before_z[z], before_x[x], s)
+        chain[0] = here
+        chain[1] = join(here, total_ref[...], s)
+        finish(2, all_y, y, along_y)
+        state[...] = jnp.concatenate(
+            [jnp.where(eye(s), var_ref[...], 0.0), jnp.broadcast_to(mean_ref[...], (PAD, s))], axis=0)
+
+        @pl.loop(0, y)
+        def _(q):
+            state[...] = join(state[...], all_y[q], 0)
+
+        own = state[...]
+        state[...] = join(own, chain[1], 0)
+        to_second().start()
+        entry_ref[...] = join(own, chain[0], 0)
+        drain(0, all_x, x, along_x)
+        drain(1, all_z, z, along_z)
+        drain(2, all_y, y, along_y)
+        to_second().wait_send()
 
 
 def entry_of(total, init_mean, init_var):
-    s = init_mean.shape[0]
-    neutral = (jnp.eye(s, dtype=f32), jnp.zeros((s,), f32), jnp.zeros((s, s), f32))
-    element = (total[:s].T, total[2 * s], total[s:2 * s])
-    inner = entering(element, "col", combine, neutral)
-    row_whole = combine(inner, element)
-    row_total = tuple(broadcast(part, "col", lax.axis_size("col") - 1) for part in row_whole)
-    outer = entering(row_total, "row", combine, neutral)
-    carry_map, carry_shift, carry_noise = combine(outer, inner)
-    mean = jnp.dot(carry_map, init_mean, precision=highest) + carry_shift
-    cov = jnp.dot(carry_map * init_var[None, :], carry_map.T, precision=highest) + carry_noise
-    return jnp.concatenate([cov, jnp.broadcast_to(mean, (PAD, s))], axis=0)
+    rows, s = total.shape
+    vmem = pl.BlockSpec(memory_space=pltpu.VMEM)
+    return pl.pallas_call(
+        scan_kernel,
+        in_specs=[vmem] * 3,
+        out_specs=vmem,
+        out_shape=jax.ShapeDtypeStruct((s + PAD, s), f32),
+        scratch_shapes=[pltpu.VMEM((4, rows, s), f32)] * 5 + [
+            pltpu.VMEM((2, rows, s), f32),
+            pltpu.VMEM((rows, s), f32),
+            pltpu.VMEM((s + PAD, s), f32),
+            pltpu.SemaphoreType.DMA((3, 6)),
+            pltpu.SemaphoreType.DMA((3, 6)),
+            pltpu.SemaphoreType.DMA((2,)),
+            pltpu.SemaphoreType.DMA((2,)),
+        ],
+        compiler_params=pltpu.CompilerParams(collective_id=0, has_side_effects=True),
+        name="scan_devices",
+    )(total, init_mean[None, :], init_var[None, :])
 
 
 def per_device(

time: 411 us -> 107 us (0.26)
  waiting for transfers between devices: 175 us -> 0 us
  matrix products: 111 us -> 0 us
  Pallas kernels: 51.5 us -> 104 us
  blocking collectives: 45.3 us -> 0 us
  between operations: 14 us -> 0.64 us
  local copies, waits for them, and re-layouts: 6.64 us -> 1.36 us
    all_gather x4 -> x0, waiting for transfers between devices: 114 us -> none  [entering(): everything = jax.tree.map(lambda part: lax.all_gather(part, axis), shard)]
    dot_general x106 -> x0, matrix products: 111 us -> none  [the longest x26 36.7 us: combine(): jnp.matmul(moved, later_map.T, precision=highest) + later_noise]
    psum x1 -> x0, waiting for transfers between devices: 59.2 us -> none  [broadcast(): return lax.psum(block, axis)]
    pallas_call x0 -> x1, Pallas kernels: none -> 52.9 us  [entry_of(): pl.pallas_call(scan_kernel, in_specs=[vmem] * 3, out_specs=vmem, out_shap...]
    all_gather x2 -> x0, blocking collectives: 30.8 us -> none  [entering(): everything = jax.tree.map(lambda part: lax.all_gather(part, axis), shard)]
    psum x1 -> x0, blocking collectives: 14.5 us -> none  [broadcast(): return lax.psum(block, axis)]
  transfers between devices with their start and end apart: 5 -> 0, of which waited for: 5 -> 0; matrix products, arithmetic and copies ran while one was open for 1% -> 0% of each run, Pallas kernels for 0% -> 0%
where the time goes in v2:
time: 107 us; the launch traced here: 106 us
  Pallas kernels  104 us (97%)
  local copies, waits for them, and re-layouts  1.36 us (1%)
    pallas_call x1, Pallas kernels, entry_of(): pl.pallas_call(scan_kernel, in_specs=[vmem] * 3, out_specs=vmem, out_shap...  52.9 us
    pallas_call x1, Pallas kernels, local_prefix(): pl.pallas_call(functools.partial(local_kernel, steps), grid=(blocks + 1,)...  42.4 us
    pallas_call x1, Pallas kernels, outputs(): pl.pallas_call(functools.partial(output_kernel, steps), grid=(count // st...  8.94 us

profile of v2, /device:TPU:1, one launch (start us, length us, event | category | flops | bytes accessed | tf_op | source)
XLA Modules:
  0.0 106.2 jit_solution(16908254880877010768)
XLA Ops:
  0.6 1.4 %copy.11.var_ref = f32[64,1]{1,0:T(8,128)} copy(f32[64,1]{0,1:T(1,128)} %bitcast.5) | data formatting | bytes 512 | tf_op jit(solution)/shard_map/broadcast_in_dim | solution.py:138
  2.0 42.4 %local_prefix.1 = (bf16[32,256,256]{2,1,0:T(8,128)(2,1)}, bf16[32,256,256]{2,1,0:T(8,128)(2,1)}, f32[32,256]{1,0:T(8,128)}, f32[32,256]{1,0:T(8,128)}, f32[528,256]{1,0:T(8,128)}) custom-call(f32[32,256]{1,0:T(8,128)} %decay_ref.1, f32[32,64]{1,0:T(8,128)} %observed_ref.1, f32[64,1]{1,0:T(8,128)} %copy.11.var_ref, bf16[32,256,256]{2,1,0:T(8,128)(2,1)} %coupling_ref.1, ...), custom_call_target="tpu_custom_call" | custom-call | tf_op jit(solution)/shard_map/local_prefix/pallas_call | solution.py:104
  44.4 52.9 %scan_devices.1.entry_ref = f32[272,256]{1,0:T(8,128)} custom-call(f32[528,256]{1,0:T(8,128)} %get-tuple-element.7.total_ref, f32[1,256]{1,0:T(1,128)} %bitcast.3, f32[1,256]{1,0:T(1,128)} %bitcast.4), custom_call_target="tpu_custom_call" | custom-call | tf_op jit(solution)/shard_map/scan_devices/pallas_call | solution.py:339
  97.3 8.9 %outputs.1 = (f32[32,256]{1,0:T(8,128)}, f32[32,256]{1,0:T(8,128)}) custom-call(f32[272,256]{1,0:T(8,128)} %scan_devices.1.entry_ref, bf16[32,256,256]{2,1,0:T(8,128)(2,1)} %get-tuple-element.8.hi_ref, bf16[32,256,256]{2,1,0:T(8,128)(2,1)} %get-tuple-element.9.lo_ref, f32[32,256]{1,0:T(8,128)} %get-tuple-element.10.diag_ref, ...), custom_call_target="tpu_custom_call" | custom-call | tf_op jit(solution)/shard_map/outputs/pallas_call | solution.py:168

commit v3 on v2

--- a/solution.py
+++ b/solution.py
@@ -10,7 +10,7 @@
 f32 = jnp.float32
 bf16 = jnp.bfloat16
 PAD = 16
-SPB = 4
+SPB = 8
 
 
 def dot_nn(a, b):
@@ -33,89 +33,90 @@
 
 
 def local_kernel(steps, decay_ref, observed_ref, var_ref, coupling_ref, map_ref, gain_ref,
-                 factor_ref, hi_ref, lo_ref, diag_ref, shift_ref, total_ref,
-                 state, e_hi, e_lo, noise, shift):
+                 factor_ref, hi_ref, lo_ref, diag_ref, shift_ref, total_ref, state, obs_var):
     i = pl.program_id(0)
     s = decay_ref.shape[1]
-    put = lax.rem(i, 2)
-    get = 1 - put
-
-    @pl.when(i <= 1)
+
+    @pl.when(i == 0)
     def _():
         unit = jnp.where(eye(s), 1.0, 0.0).astype(f32)
         state[...] = jnp.concatenate([unit, jnp.zeros((s + PAD, s), f32)], axis=0)
+        obs_var[...] = jnp.broadcast_to(var_ref[...], obs_var.shape[::-1]).T
 
     factor = factor_ref[...]
-    block = jnp.minimum(i, pl.num_programs(0) - 2)
-    for j in range(steps):
-        t = block * steps + j
+    diagonal = eye(s)
+
+    obs_gs = dot_nn(map_ref[...].reshape(-1, s), factor).astype(bf16)
+
+    def build(j):
+        t = i * steps + j
         decay = decay_ref[pl.ds(t, 1), :]
         obs_map = map_ref[j]
         gain = gain_ref[j]
         coupling = coupling_ref[j]
         gain_t = gain.T
         obs_f = (obs_map.astype(f32) * decay + dot_nn(obs_map, coupling)).astype(bf16)
-        obs_g = dot_nn(obs_map, factor).astype(bf16)
+        obs_g = obs_gs[j * obs_map.shape[0]:(j + 1) * obs_map.shape[0]]
         e = coupling.astype(f32) - dot_nn(gain_t, obs_f)
-        hi, lo = split(e)
-        e_hi[put, j] = hi
-        e_lo[put, j] = lo
+        e_hi, e_lo = split(e)
         shaped = (factor.astype(f32) - dot_nn(gain_t, obs_g)).astype(bf16)
-        weighted = (gain.astype(f32) * var_ref[...]).astype(bf16)
-        noise[put, j] = dot_nt(shaped, shaped) + dot_nn(gain_t, weighted)
+        weighted = (gain.astype(f32) * obs_var[:, 0:1]).astype(bf16)
+        noise = dot_nt(shaped, shaped) + dot_nn(gain_t, weighted)
         z_hi, z_lo = split(jnp.broadcast_to(observed_ref[pl.ds(t, 1), :], (PAD, gain.shape[0])))
-        shift[put, j] = dot_nn(z_hi, gain) + dot_nn(z_lo, gain)
-
-    block = jnp.maximum(i - 1, 0)
-    diagonal = eye(s)
-    x = state[...]
+        both = dot_nn(jnp.concatenate([z_hi, z_lo], axis=0), gain)
+        shift = both[:PAD] + both[PAD:]
+        decay_t = jnp.broadcast_to(decay, (8, s)).T[:, 0:1]
+        return t, decay, decay_t, e_hi, e_lo, noise, shift
+
+    maps = jnp.concatenate([state[:s], state[2 * s:]], axis=0)
+    n = state[s:2 * s]
+    ready = build(0)
     for j in range(steps):
-        t = block * steps + j
-        decay = decay_ref[pl.ds(t, 1), :]
-        decay_t = jnp.broadcast_to(decay, (8, s)).T[:, 0:1]
-        eh, el = e_hi[get, j], e_lo[get, j]
-        x_hi, x_lo = split(x)
-        y = x * decay + (dot_nt(x_hi, eh) + (dot_nt(x_lo, eh) + dot_nt(x_hi, el)))
-        maps, v, b = y[:s], y[s:2 * s], y[2 * s:]
+        t, decay, decay_t, e_hi, e_lo, noise, shift = ready
         m_hi, m_lo = split(maps)
-        hi_ref[j] = m_hi
-        lo_ref[j] = m_lo
-        v_hi, v_lo = split(v)
-        n = v * decay_t + noise[get, j] + (dot_nn(eh, v_hi) + (dot_nn(eh, v_lo) + dot_nn(el, v_hi)))
-        b = b + shift[get, j]
+        moved = dot_nt(jnp.concatenate([n.astype(bf16), m_hi, m_lo], axis=0), e_hi)
+        v = n * decay + moved[:s]
+        y = maps * decay + (moved[s:2 * s + PAD] + (moved[2 * s + PAD:] + dot_nt(m_hi, e_lo)))
+        b = y[s:] + shift
+        maps = jnp.concatenate([y[:s], b], axis=0)
+        o_hi, o_lo = split(y[:s])
+        hi_ref[j] = o_hi
+        lo_ref[j] = o_lo
+        shift_ref[pl.ds(t, 1), :] = b[0:1]
+        if j + 1 < steps:
+            ready = build(j + 1)
+        n = v * decay_t + noise + dot_nn(e_hi, v.astype(bf16))
         diag_ref[pl.ds(t, 1), :] = jnp.sum(jnp.where(diagonal, n, 0.0), axis=0, keepdims=True)
-        shift_ref[pl.ds(t, 1), :] = b[0:1]
-        x = jnp.concatenate([maps, n, b], axis=0)
-    state[...] = x
+    state[:s] = maps[:s]
+    state[s:2 * s] = n
+    state[2 * s:] = maps[s:]
 
     @pl.when(i == pl.num_programs(0) - 1)
     def _():
-        total_ref[...] = x
+        total_ref[...] = state[...]
 
 
 def local_prefix(decay, coupling, obs_map, gain, factor, obs_var, observed):
     count, s = decay.shape
     m = obs_map.shape[1]
     steps = SPB
-    blocks = count // steps
-    ahead = lambda i: (jnp.minimum(i, blocks - 1), 0, 0)
-    behind = lambda i: (jnp.maximum(i - 1, 0), 0, 0)
+    block = lambda i: (i, 0, 0)
     whole = lambda i: (0, 0)
     return pl.pallas_call(
         functools.partial(local_kernel, steps),
-        grid=(blocks + 1,),
+        grid=(count // steps,),
         in_specs=[
             pl.BlockSpec((count, s), whole),
             pl.BlockSpec((count, m), whole),
-            pl.BlockSpec((m, 1), whole),
-            pl.BlockSpec((steps, s, s), ahead),
-            pl.BlockSpec((steps, m, s), ahead),
-            pl.BlockSpec((steps, m, s), ahead),
+            pl.BlockSpec((1, m), whole),
+            pl.BlockSpec((steps, s, s), block),
+            pl.BlockSpec((steps, m, s), block),
+            pl.BlockSpec((steps, m, s), block),
             pl.BlockSpec((s, s), whole),
         ],
         out_specs=[
-            pl.BlockSpec((steps, s, s), behind),
-            pl.BlockSpec((steps, s, s), behind),
+            pl.BlockSpec((steps, s, s), block),
+            pl.BlockSpec((steps, s, s), block),
             pl.BlockSpec((count, s), whole),
             pl.BlockSpec((count, s), whole),
             pl.BlockSpec((2 * s + PAD, s), whole),
@@ -129,13 +130,10 @@
         ],
         scratch_shapes=[
             pltpu.VMEM((2 * s + PAD, s), f32),
-            pltpu.VMEM((2, steps, s, s), bf16),
-            pltpu.VMEM((2, steps, s, s), bf16),
-            pltpu.VMEM((2, steps, s, s), f32),
-            pltpu.VMEM((2, steps, PAD, s), f32),
+            pltpu.VMEM((m, 8), f32),
         ],
         name="local_prefix",
-    )(decay, observed, obs_var[:, None], coupling, obs_map, gain, factor)
+    )(decay, observed, obs_var[None, :], coupling, obs_map, gain, factor)
 
 
 def output_kernel(steps, entry_ref, hi_ref, lo_ref, diag_ref, shift_ref, mean_ref, var_ref, left):

time: 107 us -> 83.1 us (0.78)
  Pallas kernels: 104 us -> 82.1 us
  local copies, waits for them, and re-layouts: 1.36 us -> 0 us
    pallas_call x1, Pallas kernels: 42.4 us -> 22.1 us  [local_prefix(): pl.pallas_call(functools.partial(local_kernel, steps), grid=(count // ste...]
    pallas_call x1, Pallas kernels: 8.94 us -> 7.13 us  [outputs(): pl.pallas_call(functools.partial(output_kernel, steps), grid=(count // st...]
    broadcast_in_dim x1 -> x0, local copies, waits for them, and re-layouts: 1.36 us -> none  [local_prefix(): obs_var[:, None]]
where the time goes in v3:
time: 83.1 us; the launch traced here: 82.8 us
  Pallas kernels  82.1 us (99%)
    pallas_call x1, Pallas kernels, entry_of(): pl.pallas_call(scan_kernel, in_specs=[vmem] * 3, out_specs=vmem, out_shap...  52.9 us
    pallas_call x1, Pallas kernels, local_prefix(): pl.pallas_call(functools.partial(local_kernel, steps), grid=(count // ste...  22.1 us
    pallas_call x1, Pallas kernels, outputs(): pl.pallas_call(functools.partial(output_kernel, steps), grid=(count // st...  7.13 us

profile of v3, /device:TPU:1, one launch (start us, length us, event | category | flops | bytes accessed | tf_op | source)
XLA Modules:
  0.0 82.8 jit_solution(18442151471141723146)
XLA Ops:
  0.6 22.1 %local_prefix.1 = (bf16[32,256,256]{2,1,0:T(8,128)(2,1)}, bf16[32,256,256]{2,1,0:T(8,128)(2,1)}, f32[32,256]{1,0:T(8,128)}, f32[32,256]{1,0:T(8,128)}, f32[528,256]{1,0:T(8,128)}) custom-call(f32[32,256]{1,0:T(8,128)} %decay_ref.1, f32[32,64]{1,0:T(8,128)} %observed_ref.1, f32[1,64]{1,0:T(1,128)} %bitcast.5, bf16[32,256,256]{2,1,0:T(8,128)(2,1)} %coupling_ref.1, ...), custom_call_target="tpu_custom_call" | custom-call | tf_op jit(solution)/shard_map/local_prefix/pallas_call | solution.py:105
  22.7 52.9 %scan_devices.1.entry_ref = f32[272,256]{1,0:T(8,128)} custom-call(f32[528,256]{1,0:T(8,128)} %get-tuple-element.7.total_ref, f32[1,256]{1,0:T(1,128)} %bitcast.3, f32[1,256]{1,0:T(1,128)} %bitcast.4), custom_call_target="tpu_custom_call" | custom-call | tf_op jit(solution)/shard_map/scan_devices/pallas_call | solution.py:337
  75.6 7.1 %outputs.1 = (f32[32,256]{1,0:T(8,128)}, f32[32,256]{1,0:T(8,128)}) custom-call(f32[272,256]{1,0:T(8,128)} %scan_devices.1.entry_ref, bf16[32,256,256]{2,1,0:T(8,128)(2,1)} %get-tuple-element.8.hi_ref, bf16[32,256,256]{2,1,0:T(8,128)(2,1)} %get-tuple-element.9.lo_ref, f32[32,256]{1,0:T(8,128)} %get-tuple-element.10.diag_ref, ...), custom_call_target="tpu_custom_call" | custom-call | tf_op jit(solution)/shard_map/outputs/pallas_call | solution.py:166

commit v4 on v0

v4 whole, which is shorter than its diff:
```python
import functools

import jax
import jax.numpy as jnp
from jax import lax
from jax.experimental import pallas as pl
from jax.experimental.pallas import tpu as pltpu
from jax.sharding import PartitionSpec as P

f32 = jnp.float32
bf16 = jnp.bfloat16
PAD = 16
SPB = 4


def dot_nn(a, b):
    return lax.dot_general(a, b, (((1,), (0,)), ((), ())), preferred_element_type=f32)


def dot_nt(a, b):
    return lax.dot_general(a, b, (((1,), (1,)), ((), ())), preferred_element_type=f32)


def split(x):
    hi = x.astype(bf16)
    return hi, (x - hi.astype(f32)).astype(bf16)


def eye(n):
    row = lax.broadcasted_iota(jnp.int32, (n, n), 0)
    col = lax.broadcasted_iota(jnp.int32, (n, n), 1)
    return row == col


MESH_ID = pl.DeviceIdType.MESH


def product(a, b):
    a_hi, a_lo = split(a)
    b_hi, b_lo = split(b)
    return dot_nn(a_hi, b_hi) + (dot_nn(a_lo, b_hi) + dot_nn(a_hi, b_lo))


def moved(part, maps):
    s = maps.shape[0]
    t_hi, t_lo = split(maps)
    x_hi, x_lo = split(part)
    y = dot_nn(x_hi, t_hi) + (dot_nn(x_lo, t_hi) + dot_nn(x_hi, t_lo))
    v_hi, v_lo = split(y[:s])
    u_hi, u_lo = t_hi.T, t_lo.T
    n = dot_nn(u_hi, v_hi) + (dot_nn(u_hi, v_lo) + dot_nn(u_lo, v_hi))
    return jnp.concatenate([n, y[s:]], axis=0)


def pack(part):
    s = part.shape[1]
    h, k = s // 2, s // 4
    square = jnp.concatenate([part[h:h + k, h:], part[h + k:s, h:]], axis=1)
    return jnp.concatenate([part[:h], square, part[s:s + 8]], axis=0)


def unpack(packed):
    s = packed.shape[1]
    h, k = s // 2, s // 4
    top, square, shift = packed[:h], packed[h:h + k], packed[h + k:]
    corner = jnp.concatenate([square[:, :h], square[:, h:]], axis=0)
    low = jnp.concatenate([top[:, h:].T, corner], axis=1)
    return jnp.concatenate([top, low] + [shift] * (PAD // 8), axis=0)


def maps_kernel(steps, decay_ref, observed_ref, coupling_ref, map_ref, gain_ref,
                step_ref, maps_ref, shift_ref, total_ref, state):
    i = pl.program_id(0)
    s = decay_ref.shape[1]
    half = decay_ref.shape[0] // 2

    @pl.when(i == 0)
    def _():
        unit = jnp.where(eye(s), 1.0, 0.0).astype(f32)
        for h in range(2):
            state[h] = jnp.concatenate([unit, jnp.zeros((PAD, s), f32)], axis=0)

    def build(h, j):
        t = h * half + i * steps + j
        decay = decay_ref[pl.ds(t, 1), :]
        obs_map, gain, coupling = map_ref[h, j], gain_ref[h, j], coupling_ref[h, j]
        obs_f = (obs_map.astype(f32) * decay + dot_nn(obs_map, coupling)).astype(bf16)
        e_hi, e_lo = split(coupling.astype(f32) - dot_nn(gain.T, obs_f))
        step_ref[h, j] = e_hi
        z_hi, z_lo = split(jnp.broadcast_to(observed_ref[pl.ds(t, 1), :], (PAD, gain.shape[0])))
        both = dot_nn(jnp.concatenate([z_hi, z_lo], axis=0), gain)
        return t, decay, e_hi, e_lo, both[:PAD] + both[PAD:]

    maps = [state[0], state[1]]
    ready = [build(0, 0), build(1, 0)]
    for j in range(steps):
        for h in range(2):
            t, decay, e_hi, e_lo, shift = ready[h]
            m_hi, m_lo = split(maps[h])
            moved = dot_nt(jnp.concatenate([m_hi, m_lo], axis=0), e_hi)
            y = maps[h] * decay + (moved[:s + PAD] + (moved[s + PAD:] + dot_nt(m_hi, e_lo)))
            b = y[s:] + shift
            maps_ref[h, j] = y[:s]
            shift_ref[pl.ds(t, 1), :] = b[0:1]
            maps[h] = jnp.concatenate([y[:s], b], axis=0)
            if j + 1 < steps:
                ready[h] = build(h, j + 1)
    for h in range(2):
        state[h] = maps[h]

    @pl.when(i == pl.num_programs(0) - 1)
    def _():
        total_ref[...] = state[...]


def halves(a):
    return a.reshape((2, a.shape[0] // 2) + a.shape[1:])


def whole(i):
    return (0, 0)


def local_maps(decay, coupling, obs_map, gain, observed):
    count, s = decay.shape
    m = obs_map.shape[1]
    steps = SPB
    block = lambda i: (0, i, 0, 0)
    square = pl.BlockSpec((2, steps, s, s), block)
    flat = pl.BlockSpec((2, steps, m, s), block)
    return pl.pallas_call(
        functools.partial(maps_kernel, steps),
        grid=(count // (2 * steps),),
        in_specs=[pl.BlockSpec((count, s), whole), pl.BlockSpec((count, m), whole),
                  square, flat, flat],
        out_specs=[square, square, pl.BlockSpec((count, s), whole),
                   pl.BlockSpec((2, s + PAD, s), lambda i: (0, 0, 0))],
        out_shape=[
            jax.ShapeDtypeStruct((2, count // 2, s, s), bf16),
            jax.ShapeDtypeStruct((2, count // 2, s, s), f32),
            jax.ShapeDtypeStruct((count, s), f32),
            jax.ShapeDtypeStruct((2, s + PAD, s), f32),
        ],
        scratch_shapes=[pltpu.VMEM((2, s + PAD, s), f32)],
        name="local_maps",
    )(decay, observed, halves(coupling), halves(obs_map), halves(gain))


def scan_kernel(steps, decay_ref, var_ref, factor_ref, map_ref, gain_ref, step_ref, total_ref,
                mean0_ref, var0_ref, entry_ref, diag_ref,
                noise, obs_var, own_map, own_part, map_x, map_z, map_y, part_x, part_z, part_y,
                later, before, pair_map, pair_part, state,
                send_sem, recv_sem, pair_sem):
    i = pl.program_id(0)
    last = pl.num_programs(0) - 1
    row, col = lax.axis_index("row"), lax.axis_index("col")
    y, z = row // 4, lax.rem(row, 4)
    x, core = col // 2, lax.rem(col, 2)
    s = decay_ref.shape[1]
    half = decay_ref.shape[0] // 2

    def step(p, by):
        return lax.rem(p + by, 4)

    def along_x(by):
        return (row, step(x, by) * 2 + core)

    def along_z(by):
        return (y * 4 + step(z, by), col)

    def along_y(by):
        return (step(y, by) * 4 + z, col)

    partner = (row, x * 2 + 1 - core)

    def on_chip(source, target, k):
        return pltpu.make_async_remote_copy(
            src_ref=source, dst_ref=target, send_sem=pair_sem.at[0, k],
            recv_sem=pair_sem.at[1, k], device_id=partner, device_id_type=MESH_ID)

    def copy(level, kind, hold, p, along, by, source=0):
        slot = step(p, source)
        return pltpu.make_async_remote_copy(
            src_ref=hold.at[slot], dst_ref=hold.at[slot],
            send_sem=send_sem.at[level, kind, by - 1], recv_sem=recv_sem.at[level, kind, by - 1],
            device_id=along(by), device_id_type=MESH_ID)

    class Ring:
        def __init__(self, *what):
            self.what = what
            self.hold, self.p = what[2], what[3]

        def start(self):
            for by in (1, 3, 2):
                copy(*self.what, by).start()

        def arrived(self, by):
            copy(*self.what, by, source=4 - by).wait_recv()
            return step(self.p, 4 - by)

        def drain(self):
            for by in (1, 3, 2):
                copy(*self.what, by).wait_send()

    mx, px = Ring(0, 0, map_x, x, along_x), Ring(0, 1, part_x, x, along_x)
    mz, pz = Ring(1, 0, map_z, z, along_z), Ring(1, 1, part_z, z, along_z)
    my, py = Ring(2, 0, map_y, y, along_y), Ring(2, 1, part_y, y, along_y)

    @pl.when(i == 0)
    def _():
        barrier = pltpu.get_barrier_semaphore()
        pl.semaphore_signal(barrier, inc=1, device_id=partner, device_id_type=MESH_ID)
        for along in (along_x, along_z, along_y):
            for by in (1, 2, 3):
                pl.semaphore_signal(barrier, inc=1, device_id=along(by), device_id_type=MESH_ID)
        noise[...] = jnp.zeros_like(noise)
        obs_var[...] = jnp.broadcast_to(var_ref[...], obs_var.shape[::-1]).T
        own_map[...] = product(total_ref[0, :s], total_ref[1, :s])
        pl.semaphore_wait(barrier, 10)

        @pl.when(core == 1)
        def _():
            on_chip(own_map, pair_map, 0).start()

    @pl.when(jnp.logical_and(i == 0, core == 0))
    def _():
        on_chip(own_map, pair_map, 0).wait_recv()
        map_x[x] = product(own_map[...], pair_map[...])
        mx.start()

    factor = factor_ref[...]
    diagonal = eye(s)
    m = map_ref.shape[2]
    obs_gs = dot_nn(map_ref[...].reshape(-1, s), factor).astype(bf16)

    def build(h, j):
        t = h * half + i * steps + j
        gain = gain_ref[h, j]
        gain_t = gain.T
        k = h * steps + j
        shaped = (factor.astype(f32) - dot_nn(gain_t, obs_gs[k * m:(k + 1) * m])).astype(bf16)
        weighted = (gain.astype(f32) * obs_var[:, 0:1]).astype(bf16)
        decay = decay_ref[pl.ds(t, 1), :]
        decay_t = jnp.broadcast_to(decay, (8, s)).T[:, 0:1]
        return t, decay, decay_t, dot_nt(shaped, shaped) + dot_nn(gain_t, weighted)

    ns = [noise[0], noise[1]]
    ready = [build(0, 0), build(1, 0)]
    for j in range(steps):
        for h in range(2):
            t, decay, decay_t, fresh = ready[h]
            e = step_ref[h, j]
            v = ns[h] * decay + dot_nt(ns[h].astype(bf16), e)
            if j + 1 < steps:
                ready[h] = build(h, j + 1)
            n = v * decay_t + fresh + dot_nn(e, v.astype(bf16))
            diag_ref[pl.ds(t, 1), :] = jnp.sum(jnp.where(diagonal, n, 0.0), axis=0, keepdims=True)
            ns[h] = n
    for h in range(2):
        noise[h] = ns[h]

    def pairs(maps):
        m01 = product(maps[0], maps[1])
        m23 = product(maps[2], maps[3])
        return m01, m23

    def suffixes(maps, m23):
        later[3] = jnp.where(eye(s), 1.0, 0.0).astype(f32)
        later[2] = maps[3]
        later[1] = m23
        later[0] = product(maps[1], m23)

    def earlier_map(p, maps, m01):
        m012 = product(m01, maps[2])
        unit = jnp.where(eye(s), 1.0, 0.0).astype(f32)
        low = jnp.where(p == 0, unit, maps[0])
        return jnp.where(p < 2, low, jnp.where(p == 2, m01, m012))

    def earlier_part(p, parts, maps):
        p0 = unpack(parts[0])
        p01 = moved(p0, maps[1]) + unpack(parts[1])
        p012 = moved(p01, maps[2]) + unpack(parts[2])
        low = jnp.where(p == 0, 0.0, p0)
        return jnp.where(p < 2, low, jnp.where(p == 2, p01, p012))

    def total_part(ring, p):
        parts = ring.hold
        sum_ = moved(unpack(parts[p]), later[p])
        left, right = ring.arrived(1), ring.arrived(3)
        sum_ = sum_ + moved(unpack(parts[left]), later[left])
        sum_ = sum_ + moved(unpack(parts[right]), later[right])
        across = ring.arrived(2)
        return pack(sum_ + moved(unpack(parts[across]), later[across]))

    def first_half():
        return jnp.concatenate([noise[0], total_ref[0, s:]], axis=0)

    @pl.when(i == last)
    def _():
        second = jnp.concatenate([noise[1], total_ref[1, s:]], axis=0)
        own_part[...] = moved(first_half(), total_ref[1, :s]) + second

    @pl.when(jnp.logical_and(i == last, core == 1))
    def _():
        on_chip(own_part, pair_part, 1).start()
        on_chip(own_map, pair_map, 0).wait_send()
        on_chip(own_part, pair_part, 1).wait_send()
        on_chip(state, state, 2).wait_recv()
        entry = unpack(state[...])
        entry_ref[0] = entry
        entry_ref[1] = moved(entry, total_ref[0, :s]) + first_half()

    @pl.when(jnp.logical_and(i == last, core == 0))
    def _():
        for by in (1, 3, 2):
            mx.arrived(by)
        x01, x23 = pairs(map_x)
        map_z[z] = product(x01, x23)
        mz.start()
        on_chip(own_part, pair_part, 1).wait_recv()
        part_x[x] = pack(moved(own_part[...], pair_map[...]) + pair_part[...])
        px.start()
        suffixes(map_x, x23)
        before[0] = earlier_map(x, map_x, x01)
        part_z[z] = total_part(px, x)
        pz.start()
        for by in (1, 3, 2):
            mz.arrived(by)
        z01, z23 = pairs(map_z)
        map_y[y] = product(z01, z23)
        my.start()
        suffixes(map_z, z23)
        near = earlier_part(x, part_x, map_x)
        before[3] = product(earlier_map(z, map_z, z01), before[0])
        part_y[y] = total_part(pz, z)
        py.start()
        near = near + moved(earlier_part(z, part_z, map_z), before[0])
        for by in (1, 3, 2):
            my.arrived(by)
        for q in (2, 1, 0):
            after = before[q + 1]
            before[q] = jnp.where(q < y, product(map_y[q], after), after)
        t0 = before[0]
        weights = jnp.broadcast_to(var0_ref[...], (8, s)).T[:, 0:1]
        u_hi, u_lo = split(t0)
        w_hi, w_lo = split(t0 * weights)
        u_hi_t, u_lo_t = u_hi.T, u_lo.T
        start_noise = dot_nn(u_hi_t, w_hi) + (dot_nn(u_hi_t, w_lo) + dot_nn(u_lo_t, w_hi))
        start_mean = product(jnp.broadcast_to(mean0_ref[...], (PAD, s)), t0)
        near = near + jnp.concatenate([start_noise, start_mean], axis=0)
        for by in (1, 3, 2):
            q = py.arrived(by)
            part = moved(unpack(part_y[q]), before[jnp.minimum(q + 1, 3)])
            near = near + jnp.where(q < y, part, 0.0)
        state[...] = pack(moved(near, own_map[...]) + own_part[...])
        on_chip(state, state, 2).start()
        entry_ref[0] = near
        entry_ref[1] = moved(near, total_ref[0, :s]) + first_half()
        for ring in (mx, px, mz, pz, my, py):
            ring.drain()
        on_chip(state, state, 2).wait_send()


def scan(decay, obs_var, factor, obs_map, gain, step_maps, total, init_mean, init_var):
    count, s = decay.shape
    m = obs_map.shape[1]
    steps = SPB
    rows = s + PAD
    packed = s // 2 + s // 4 + 8
    block = lambda i: (0, i, 0, 0)
    flat = pl.BlockSpec((2, steps, m, s), block)
    three = lambda i: (0, 0, 0)
    return pl.pallas_call(
        functools.partial(scan_kernel, steps),
        grid=(count // (2 * steps),),
        in_specs=[
            pl.BlockSpec((count, s), whole),
            pl.BlockSpec((1, m), whole),
            pl.BlockSpec((s, s), whole),
            flat,
            flat,
            pl.BlockSpec((2, steps, s, s), block),
            pl.BlockSpec((2, rows, s), three),
            pl.BlockSpec((1, s), whole),
            pl.BlockSpec((1, s), whole),
        ],
        out_specs=[pl.BlockSpec((2, rows, s), three), pl.BlockSpec((count, s), whole)],
        out_shape=[
            jax.ShapeDtypeStruct((2, rows, s), f32),
            jax.ShapeDtypeStruct((count, s), f32),
        ],
        scratch_shapes=[
            pltpu.VMEM((2, s, s), f32),
            pltpu.VMEM((m, 8), f32),
            pltpu.VMEM((s, s), f32),
            pltpu.VMEM((rows, s), f32),
        ] + [pltpu.VMEM((4, s, s), f32)] * 3 + [pltpu.VMEM((4, packed, s), f32)] * 3 + [
            pltpu.VMEM((4, s, s), f32),
            pltpu.VMEM((4, s, s), f32),
            pltpu.VMEM((s, s), f32),
            pltpu.VMEM((rows, s), f32),
            pltpu.VMEM((packed, s), f32),
            pltpu.SemaphoreType.DMA((3, 2, 3)),
            pltpu.SemaphoreType.DMA((3, 2, 3)),
            pltpu.SemaphoreType.DMA((2, 3)),
        ],
        compiler_params=pltpu.CompilerParams(collective_id=0, has_side_effects=True),
        name="scan_devices",
    )(decay, obs_var[None, :], factor, halves(obs_map), halves(gain), step_maps, total,
      init_mean[None, :], init_var[None, :])


def output_kernel(steps, entry_ref, maps_ref, diag_ref, shift_ref, mean_ref, var_ref,
                  off, straight, first_mean):
    i = pl.program_id(0)
    s = maps_ref.shape[3]
    half = diag_ref.shape[0] // 2

    @pl.when(i == 0)
    def _():
        diagonal = eye(s)
        for h in range(2):
            cov = entry_ref[h, :s]
            off[h] = jnp.where(diagonal, 0.0, cov).astype(bf16)
            held = jnp.sum(jnp.where(diagonal, cov, 0.0), axis=1, keepdims=True)
            straight[h] = jnp.broadcast_to(held, (s, s))
            first_mean[h] = jnp.broadcast_to(entry_ref[h, s:s + 8].T[:, 0:1], (s, s))

    for j in range(steps):
        for h in range(2):
            t = h * half + i * steps + j
            maps = maps_ref[h, j]
            r = dot_nn(off[h], maps.astype(bf16)) + straight[h] * maps
            var_ref[pl.ds(t, 1), :] = (
                jnp.sum(r * maps, axis=0, keepdims=True) + diag_ref[pl.ds(t, 1), :]
            )
            mean_ref[pl.ds(t, 1), :] = (
                jnp.sum(first_mean[h] * maps, axis=0, keepdims=True) + shift_ref[pl.ds(t, 1), :]
            )


def outputs(entry, maps, diag, shift):
    count, s = diag.shape
    steps = SPB
    full = pl.BlockSpec((count, s), whole)
    return pl.pallas_call(
        functools.partial(output_kernel, steps),
        grid=(count // (2 * steps),),
        in_specs=[
            pl.BlockSpec((2, s + PAD, s), lambda i: (0, 0, 0)),
            pl.BlockSpec((2, steps, s, s), lambda i: (0, i, 0, 0)),
            full,
            full,
        ],
        out_specs=[full, full],
        out_shape=[jax.ShapeDtypeStruct((count, s), f32)] * 2,
        scratch_shapes=[
            pltpu.VMEM((2, s, s), bf16),
            pltpu.VMEM((2, s, s), f32),
            pltpu.VMEM((2, s, s), f32),
        ],
        name="outputs",
    )(entry, maps, diag, shift)


def per_device(
    init_mean, init_var, decay, coupling, obs_map, gain, noise_factor, obs_var, observed
):
    step_maps, maps, shift, total = local_maps(decay, coupling, obs_map, gain, observed)
    entry, diag = scan(
        decay, obs_var, noise_factor, obs_map, gain, step_maps, total, init_mean, init_var
    )
    means, variances = outputs(entry, maps, diag, shift)
    return (means, variances)


def solution(mesh):
    return jax.shard_map(
        per_device,
        mesh=mesh,
        in_specs=(
            P(),
            P(),
            P(("row", "col"), None),
            P(("row", "col"), None, None),
            P(("row", "col"), None, None),
            P(("row", "col"), None, None),
            P(),
            P(),
            P(("row", "col"), None),
        ),
        out_specs=(P(("row", "col"), None), P(("row", "col"), None)),
        check_vma=False,
    )
```

time: 892 us -> 70.5 us (0.08); the launches traced: 880 us -> 70.2 us
  matrix products: 454 us -> 0 us
  local copies, waits for them, and re-layouts: 182 us -> 0 us
  waiting for transfers between devices: 177 us -> 0 us
  Pallas kernels: 0 us -> 69.6 us
  blocking collectives: 45.5 us -> 0 us
  between operations: 14.1 us -> 0.64 us
    dot_general x335 -> x0, matrix products: 454 us -> none  [the longest x58 83.6 us: combine(): jnp.matmul(moved, jnp.swapaxes(later_map, -1, -2), precision=highest)]
    all_gather x4 -> x0, waiting for transfers between devices: 117 us -> none  [entering(): everything = jax.tree.map(lambda part: lax.all_gather(part, axis), shard)]
    dynamic_update_slice x64 -> x0, local copies, waits for them, and re-layouts: 84.2 us -> none  [per_device(): lax.scan(advance, (entry_mean, entry_cov), (step_map, shift, noise))]
    gather x32 -> x0, local copies, waits for them, and re-layouts: 75 us -> none  [advance(): return ((state_mean, state_cov), (state_mean, jnp.diagonal(state_cov)))]
    pallas_call x0 -> x3, Pallas kernels: none -> 69.6 us  [the longest x1 50.6 us: scan(): pl.pallas_call(functools.partial(scan_kernel, steps), grid=(count // (2 *...]
    psum x1 -> x0, waiting for transfers between devices: 59.2 us -> none  [broadcast(): return lax.psum(block, axis)]
    all_gather x2 -> x0, blocking collectives: 30.9 us -> none  [entering(): everything = jax.tree.map(lambda part: lax.all_gather(part, axis), shard)]
    unnamed x38 -> x0, local copies, waits for them, and re-layouts: 16.4 us -> none
  transfers between devices with their start and end apart: 5 -> 0, of which waited for: 5 -> 0; matrix products, arithmetic and copies ran while one was open for 0% -> 0% of each run, Pallas kernels for 0% -> 0%
where the time goes in v4:
time: 70.5 us; the launch traced here: 70.2 us
  Pallas kernels  69.6 us (99%)
    pallas_call x1, Pallas kernels, scan(): pl.pallas_call(functools.partial(scan_kernel, steps), grid=(count // (2 *...  50.6 us
    pallas_call x1, Pallas kernels, local_maps(): pl.pallas_call(functools.partial(maps_kernel, steps), grid=(count // (2 *...  12.7 us
    pallas_call x1, Pallas kernels, outputs(): pl.pallas_call(functools.partial(output_kernel, steps), grid=(count // (2...  6.24 us

profile of v4, /device:TPU:1, one launch (start us, length us, event | category | flops | bytes accessed | tf_op | source)
XLA Modules:
  0.0 70.2 jit_solution(18354212484400878739)
XLA Ops:
  0.6 12.7 %local_maps.1 = (bf16[2,16,256,256]{3,2,1,0:T(8,128)(2,1)}, f32[2,16,256,256]{3,2,1,0:T(8,128)}, f32[32,256]{1,0:T(8,128)}, f32[2,272,256]{2,1,0:T(8,128)}) custom-call(f32[32,256]{1,0:T(8,128)} %decay_ref.3, f32[32,64]{1,0:T(8,128)} %observed_ref.1, bf16[2,16,256,256]{3,2,1,0:T(8,128)(2,1)} %bitcast.6, bf16[2,16,64,256]{3,2,1,0:T(8,128)(2,1)} %bitcast.7, ...), custom_call_target="tpu_custom_call" | custom-call | tf_op jit(solution)/shard_map/local_maps/pallas_call | solution.py:131
  13.4 50.6 %scan_devices.1 = (f32[2,272,256]{2,1,0:T(8,128)}, f32[32,256]{1,0:T(8,128)}) custom-call(f32[32,256]{1,0:T(8,128)} %decay_ref.3, f32[1,64]{1,0:T(1,128)} %bitcast.13, bf16[256,256]{1,0:T(8,128)(2,1)} %factor_ref.1, bf16[2,16,64,256]{3,2,1,0:T(8,128)(2,1)} %bitcast.8, bf16[2,16,64,256]{3,2,1,0:T(8,128)(2,1)} %bitcast.10, ...), custom_call_target="tpu_custom_call" | custom-call | tf_op jit(solution)/shard_map/scan_devices/pallas_call | solution.py:373
  64.0 6.2 %outputs.1 = (f32[32,256]{1,0:T(8,128)}, f32[32,256]{1,0:T(8,128)}) custom-call(f32[2,272,256]{2,1,0:T(8,128)} %get-tuple-element.10.entry_ref, f32[2,16,256,256]{3,2,1,0:T(8,128)} %get-tuple-element.11.maps_ref, f32[32,256]{1,0:T(8,128)} %get-tuple-element.12.diag_ref, f32[32,256]{1,0:T(8,128)} %get-tuple-element.13.shift_ref), custom_call_target="tpu_custom_call" | custom-call | tf_op jit(solution)/shard_map/outputs/pallas_call | solution.py:446

commit v5 on v4

--- a/solution.py
+++ b/solution.py
@@ -147,10 +147,11 @@
 
 
 def scan_kernel(steps, decay_ref, var_ref, factor_ref, map_ref, gain_ref, step_ref, total_ref,
-                mean0_ref, var0_ref, entry_ref, diag_ref,
-                noise, obs_var, own_map, own_part, map_x, map_z, map_y, part_x, part_z, part_y,
-                later, before, pair_map, pair_part, state,
-                send_sem, recv_sem, pair_sem):
+                mean0_ref, var0_ref, shift_ref, maps_ref, mean_ref, out_ref,
+                noise, obs_var, base, base_half, diag, own_map, own_part,
+                map_x, map_z, map_y, part_x, part_z, part_y,
+                later, before, pair_map, pair_part, state, entry, maps_here, off, straight,
+                first_mean, send_sem, recv_sem, pair_sem, maps_sem):
     i = pl.program_id(0)
     last = pl.num_programs(0) - 1
     row, col = lax.axis_index("row"), lax.axis_index("col")
@@ -214,47 +215,55 @@
             for by in (1, 2, 3):
                 pl.semaphore_signal(barrier, inc=1, device_id=along(by), device_id_type=MESH_ID)
         noise[...] = jnp.zeros_like(noise)
-        obs_var[...] = jnp.broadcast_to(var_ref[...], obs_var.shape[::-1]).T
+        obs_var[...] = jnp.broadcast_to(var_ref[...] * 0.5, obs_var.shape[::-1]).T
         own_map[...] = product(total_ref[0, :s], total_ref[1, :s])
+        q = dot_nt(factor_ref[...], factor_ref[...])
+        base[...] = q
+        base_half[...] = q.astype(bf16)
         pl.semaphore_wait(barrier, 10)
-
-        @pl.when(core == 1)
-        def _():
-            on_chip(own_map, pair_map, 0).start()
-
-    @pl.when(jnp.logical_and(i == 0, core == 0))
-    def _():
+        on_chip(own_map, pair_map, 0).start()
+
+    fetch = pltpu.make_async_copy(maps_ref, maps_here, maps_sem.at[0])
+
+    @pl.when(i == 1)
+    def _():
+        fetch.start()
         on_chip(own_map, pair_map, 0).wait_recv()
+
+    @pl.when(jnp.logical_and(i == 1, core == 0))
+    def _():
         map_x[x] = product(own_map[...], pair_map[...])
         mx.start()
 
-    factor = factor_ref[...]
     diagonal = eye(s)
     m = map_ref.shape[2]
-    obs_gs = dot_nn(map_ref[...].reshape(-1, s), factor).astype(bf16)
+    seen_all = dot_nn(map_ref[...].reshape(-1, s), base_half[...])
 
     def build(h, j):
         t = h * half + i * steps + j
-        gain = gain_ref[h, j]
-        gain_t = gain.T
         k = h * steps + j
-        shaped = (factor.astype(f32) - dot_nn(gain_t, obs_gs[k * m:(k + 1) * m])).astype(bf16)
-        weighted = (gain.astype(f32) * obs_var[:, 0:1]).astype(bf16)
+        obs_map, gain = map_ref[h, j], gain_ref[h, j]
+        seen = seen_all[k * m:(k + 1) * m]
+        inner = (dot_nt(obs_map, seen.astype(bf16)) * 0.5).astype(bf16)
+        fresh = (dot_nn(inner, gain) + gain.astype(f32) * obs_var[:, 0:1] - seen).astype(bf16)
         decay = decay_ref[pl.ds(t, 1), :]
         decay_t = jnp.broadcast_to(decay, (8, s)).T[:, 0:1]
-        return t, decay, decay_t, dot_nt(shaped, shaped) + dot_nn(gain_t, weighted)
+        left = jnp.concatenate([gain, fresh], axis=0).T
+        return t, decay, decay_t, left, jnp.concatenate([fresh, gain], axis=0)
 
     ns = [noise[0], noise[1]]
     ready = [build(0, 0), build(1, 0)]
     for j in range(steps):
         for h in range(2):
-            t, decay, decay_t, fresh = ready[h]
+            t, decay, decay_t, left, right = ready[h]
             e = step_ref[h, j]
             v = ns[h] * decay + dot_nt(ns[h].astype(bf16), e)
             if j + 1 < steps:
                 ready[h] = build(h, j + 1)
-            n = v * decay_t + fresh + dot_nn(e, v.astype(bf16))
-            diag_ref[pl.ds(t, 1), :] = jnp.sum(jnp.where(diagonal, n, 0.0), axis=0, keepdims=True)
+            pushed = dot_nn(jnp.concatenate([e, left], axis=1),
+                            jnp.concatenate([v.astype(bf16), right], axis=0))
+            n = v * decay_t + base[...] + pushed
+            diag[pl.ds(t, 1), :] = jnp.sum(jnp.where(diagonal, n, 0.0), axis=0, keepdims=True)
             ns[h] = n
     for h in range(2):
         noise[h] = ns[h]
@@ -295,20 +304,21 @@
     def first_half():
         return jnp.concatenate([noise[0], total_ref[0, s:]], axis=0)
 
-    @pl.when(i == last)
-    def _():
-        second = jnp.concatenate([noise[1], total_ref[1, s:]], axis=0)
-        own_part[...] = moved(first_half(), total_ref[1, :s]) + second
+    def second_half():
+        return jnp.concatenate([noise[1], total_ref[1, s:]], axis=0)
 
     @pl.when(jnp.logical_and(i == last, core == 1))
     def _():
+        own_part[...] = moved(first_half(), total_ref[1, :s]) + second_half()
         on_chip(own_part, pair_part, 1).start()
-        on_chip(own_map, pair_map, 0).wait_send()
-        on_chip(own_part, pair_part, 1).wait_send()
+        before[0] = product(pair_map[...], total_ref[0, :s])
+        on_chip(own_part, pair_part, 1).wait_recv()
+        part = pair_part[...]
+        kept = moved(part, total_ref[0, :s]) + first_half()
         on_chip(state, state, 2).wait_recv()
-        entry = unpack(state[...])
-        entry_ref[0] = entry
-        entry_ref[1] = moved(entry, total_ref[0, :s]) + first_half()
+        near = unpack(state[...])
+        entry[0] = moved(near, pair_map[...]) + pair_part[...]
+        entry[1] = moved(near, before[0]) + kept
 
     @pl.when(jnp.logical_and(i == last, core == 0))
     def _():
@@ -317,10 +327,14 @@
         x01, x23 = pairs(map_x)
         map_z[z] = product(x01, x23)
         mz.start()
+        far = product(total_ref[1, :s], pair_map[...])
+        mine = moved(first_half(), far) + moved(second_half(), pair_map[...])
         on_chip(own_part, pair_part, 1).wait_recv()
-        part_x[x] = pack(moved(own_part[...], pair_map[...]) + pair_part[...])
+        part_x[x] = pack(mine + pair_part[...])
         px.start()
         suffixes(map_x, x23)
+        own_part[...] = moved(first_half(), total_ref[1, :s]) + second_half()
+        on_chip(own_part, pair_part, 1).start()
         before[0] = earlier_map(x, map_x, x01)
         part_z[z] = total_part(px, x)
         pz.start()
@@ -352,16 +366,48 @@
             q = py.arrived(by)
             part = moved(unpack(part_y[q]), before[jnp.minimum(q + 1, 3)])
             near = near + jnp.where(q < y, part, 0.0)
-        state[...] = pack(moved(near, own_map[...]) + own_part[...])
+        state[...] = pack(near)
         on_chip(state, state, 2).start()
-        entry_ref[0] = near
-        entry_ref[1] = moved(near, total_ref[0, :s]) + first_half()
+        entry[0] = near
+        entry[1] = moved(near, total_ref[0, :s]) + first_half()
+
+    @pl.when(i == last)
+    def _():
+        for h in range(2):
+            cov = entry[h, :s]
+            off[h] = jnp.where(diagonal, 0.0, cov).astype(bf16)
+            held = jnp.sum(jnp.where(diagonal, cov, 0.0), axis=1, keepdims=True)
+            straight[h] = jnp.broadcast_to(held, (s, s))
+            first_mean[h] = jnp.broadcast_to(entry[h, s:s + 8].T[:, 0:1], (s, s))
+        fetch.wait()
+
+        @pl.loop(0, half // steps)
+        def _(block):
+            for j in range(steps):
+                for h in range(2):
+                    k = block * steps + j
+                    t = h * half + k
+                    maps = maps_here[h, k]
+                    r = dot_nn(off[h], maps.astype(bf16)) + straight[h] * maps
+                    out_ref[pl.ds(t, 1), :] = (
+                        jnp.sum(r * maps, axis=0, keepdims=True) + diag[pl.ds(t, 1), :]
+                    )
+                    mean_ref[pl.ds(t, 1), :] = (
+                        jnp.sum(first_mean[h] * maps, axis=0, keepdims=True)
+                        + shift_ref[pl.ds(t, 1), :]
+                    )
+
+        on_chip(own_map, pair_map, 0).wait_send()
+        on_chip(own_part, pair_part, 1).wait_send()
+
+    @pl.when(jnp.logical_and(i == last, core == 0))
+    def _():
         for ring in (mx, px, mz, pz, my, py):
             ring.drain()
         on_chip(state, state, 2).wait_send()
 
 
-def scan(decay, obs_var, factor, obs_map, gain, step_maps, total, init_mean, init_var):
+def scan(decay, obs_var, factor, obs_map, gain, step_maps, total, init_mean, init_var, shift, maps):
     count, s = decay.shape
     m = obs_map.shape[1]
     steps = SPB
@@ -383,15 +429,17 @@
             pl.BlockSpec((2, rows, s), three),
             pl.BlockSpec((1, s), whole),
             pl.BlockSpec((1, s), whole),
+            pl.BlockSpec((count, s), whole),
+            pl.BlockSpec(memory_space=pl.ANY),
         ],
-        out_specs=[pl.BlockSpec((2, rows, s), three), pl.BlockSpec((count, s), whole)],
-        out_shape=[
-            jax.ShapeDtypeStruct((2, rows, s), f32),
-            jax.ShapeDtypeStruct((count, s), f32),
-        ],
+        out_specs=[pl.BlockSpec((count, s), whole)] * 2,
+        out_shape=[jax.ShapeDtypeStruct((count, s), f32)] * 2,
         scratch_shapes=[
             pltpu.VMEM((2, s, s), f32),
             pltpu.VMEM((m, 8), f32),
+            pltpu.VMEM((s, s), f32),
+            pltpu.VMEM((s, s), bf16),
+            pltpu.VMEM((count, s), f32),
             pltpu.VMEM((s, s), f32),
             pltpu.VMEM((rows, s), f32),
         ] + [pltpu.VMEM((4, s, s), f32)] * 3 + [pltpu.VMEM((4, packed, s), f32)] * 3 + [
@@ -400,77 +448,30 @@
             pltpu.VMEM((s, s), f32),
             pltpu.VMEM((rows, s), f32),
             pltpu.VMEM((packed, s), f32),
+            pltpu.VMEM((2, rows, s), f32),
+            pltpu.VMEM((2, count // 2, s, s), f32),
+            pltpu.VMEM((2, s, s), bf16),
+            pltpu.VMEM((2, s, s), f32),
+            pltpu.VMEM((2, s, s), f32),
             pltpu.SemaphoreType.DMA((3, 2, 3)),
             pltpu.SemaphoreType.DMA((3, 2, 3)),
             pltpu.SemaphoreType.DMA((2, 3)),
+            pltpu.SemaphoreType.DMA((1,)),
         ],
         compiler_params=pltpu.CompilerParams(collective_id=0, has_side_effects=True),
         name="scan_devices",
     )(decay, obs_var[None, :], factor, halves(obs_map), halves(gain), step_maps, total,
-      init_mean[None, :], init_var[None, :])
-
-
-def output_kernel(steps, entry_ref, maps_ref, diag_ref, shift_ref, mean_ref, var_ref,
-                  off, straight, first_mean):
-    i = pl.program_id(0)
-    s = maps_ref.shape[3]
-    half = diag_ref.shape[0] // 2
-
-    @pl.when(i == 0)
-    def _():
-        diagonal = eye(s)
-        for h in range(2):
-            cov = entry_ref[h, :s]
-            off[h] = jnp.where(diagonal, 0.0, cov).astype(bf16)
-            held = jnp.sum(jnp.where(diagonal, cov, 0.0), axis=1, keepdims=True)
-            straight[h] = jnp.broadcast_to(held, (s, s))
-            first_mean[h] = jnp.broadcast_to(entry_ref[h, s:s + 8].T[:, 0:1], (s, s))
-
-    for j in range(steps):
-        for h in range(2):
-            t = h * half + i * steps + j
-            maps = maps_ref[h, j]
-            r = dot_nn(off[h], maps.astype(bf16)) + straight[h] * maps
-            var_ref[pl.ds(t, 1), :] = (
-                jnp.sum(r * maps, axis=0, keepdims=True) + diag_ref[pl.ds(t, 1), :]
-            )
-            mean_ref[pl.ds(t, 1), :] = (
-                jnp.sum(first_mean[h] * maps, axis=0, keepdims=True) + shift_ref[pl.ds(t, 1), :]
-            )
-
-
-def outputs(entry, maps, diag, shift):
-    count, s = diag.shape
-    steps = SPB
-    full = pl.BlockSpec((count, s), whole)
-    return pl.pallas_call(
-        functools.partial(output_kernel, steps),
-        grid=(count // (2 * steps),),
-        in_specs=[
-            pl.BlockSpec((2, s + PAD, s), lambda i: (0, 0, 0)),
-            pl.BlockSpec((2, steps, s, s), lambda i: (0, i, 0, 0)),
-            full,
-            full,
-        ],
-        out_specs=[full, full],
-        out_shape=[jax.ShapeDtypeStruct((count, s), f32)] * 2,
-        scratch_shapes=[
-            pltpu.VMEM((2, s, s), bf16),
-            pltpu.VMEM((2, s, s), f32),
-            pltpu.VMEM((2, s, s), f32),
-        ],
-        name="outputs",
-    )(entry, maps, diag, shift)
+      init_mean[None, :], init_var[None, :], shift, maps)
 
 
 def per_device(
     init_mean, init_var, decay, coupling, obs_map, gain, noise_factor, obs_var, observed
 ):
     step_maps, maps, shift, total = local_maps(decay, coupling, obs_map, gain, observed)
-    entry, diag = scan(
-        decay, obs_var, noise_factor, obs_map, gain, step_maps, total, init_mean, init_var
+    means, variances = scan(
+        decay, obs_var, noise_factor, obs_map, gain, step_maps, total, init_mean, init_var,
+        shift, maps,
     )
-    means, variances = outputs(entry, maps, diag, shift)
     return (means, variances)
 
 

time: 70.5 us -> 72.8 us (1.033)
  local copies, waits for them, and re-layouts: 0 us -> 2.75 us
    pallas_call x1 -> x0, Pallas kernels: 6.24 us -> none  [outputs(): pl.pallas_call(functools.partial(output_kernel, steps), grid=(count // (2...]
    pallas_call x1, Pallas kernels: 50.6 us -> 56.3 us  [scan(): pl.pallas_call(functools.partial(scan_kernel, steps), grid=(count // (2 *...]
    unnamed x0 -> x2, local copies, waits for them, and re-layouts: none -> 2.75 us
where the time goes in v5:
time: 72.8 us; the launch traced here: 72.5 us
  Pallas kernels  69.1 us (95%)
  local copies, waits for them, and re-layouts  2.75 us (4%)
    pallas_call x1, Pallas kernels, scan(): pl.pallas_call(functools.partial(scan_kernel, steps), grid=(count // (2 *...  56.3 us
    pallas_call x1, Pallas kernels, local_maps(): pl.pallas_call(functools.partial(maps_kernel, steps), grid=(count // (2 *...  12.8 us
    unnamed x2, local copies, waits for them, and re-layouts  2.75 us

profile of v5, /device:TPU:1, one launch (start us, length us, event | category | flops | bytes accessed | tf_op | source)
XLA Modules:
  0.0 72.5 jit_solution(8519259558504781797)
XLA Ops:
  0.6 12.8 %local_maps.1 = (bf16[2,16,256,256]{3,2,1,0:T(8,128)(2,1)}, f32[2,16,256,256]{3,2,1,0:T(8,128)}, f32[32,256]{1,0:T(8,128)}, f32[2,272,256]{2,1,0:T(8,128)}) custom-call(f32[32,256]{1,0:T(8,128)} %decay_ref.3, f32[32,64]{1,0:T(8,128)} %observed_ref.1, bf16[2,16,256,256]{3,2,1,0:T(8,128)(2,1)} %bitcast.6, bf16[2,16,64,256]{3,2,1,0:T(8,128)(2,1)} %bitcast.7, ...), custom_call_target="tpu_custom_call" | custom-call | tf_op jit(solution)/shard_map/local_maps/pallas_call | solution.py:131
  13.4 56.3 %scan_devices.1 = (f32[32,256]{1,0:T(8,128)}, f32[32,256]{1,0:T(8,128)}) custom-call(f32[32,256]{1,0:T(8,128)} %decay_ref.3, f32[1,64]{1,0:T(1,128)} %bitcast.13, bf16[256,256]{1,0:T(8,128)(2,1)} %factor_ref.1, bf16[2,16,64,256]{3,2,1,0:T(8,128)(2,1)} %bitcast.8, bf16[2,16,64,256]{3,2,1,0:T(8,128)(2,1)} %bitcast.10, ...), custom_call_target="tpu_custom_call" | custom-call | tf_op jit(solution)/shard_map/scan_devices/pallas_call | solution.py:419
  69.7 1.4 %copy.13 = f32[32,256]{1,0:T(8,128)} copy(f32[32,256]{1,0:T(8,128)} %get-tuple-element.12) | data formatting | bytes 65536
  71.1 1.4 %copy.14 = f32[32,256]{1,0:T(8,128)} copy(f32[32,256]{1,0:T(8,128)} %get-tuple-element.13) | data formatting | bytes 65536

commit v6 on v5

--- a/solution.py
+++ b/solution.py
@@ -147,7 +147,7 @@
 
 
 def scan_kernel(steps, decay_ref, var_ref, factor_ref, map_ref, gain_ref, step_ref, total_ref,
-                mean0_ref, var0_ref, shift_ref, maps_ref, mean_ref, out_ref,
+                mean0_ref, var0_ref, shift_ref, maps_ref, out_ref,
                 noise, obs_var, base, base_half, diag, own_map, own_part,
                 map_x, map_z, map_y, part_x, part_z, part_y,
                 later, before, pair_map, pair_part, state, entry, maps_here, off, straight,
@@ -179,29 +179,54 @@
             src_ref=source, dst_ref=target, send_sem=pair_sem.at[0, k],
             recv_sem=pair_sem.at[1, k], device_id=partner, device_id_type=MESH_ID)
 
-    def copy(level, kind, hold, p, along, by, source=0):
-        slot = step(p, source)
-        return pltpu.make_async_remote_copy(
-            src_ref=hold.at[slot], dst_ref=hold.at[slot],
-            send_sem=send_sem.at[level, kind, by - 1], recv_sem=recv_sem.at[level, kind, by - 1],
-            device_id=along(by), device_id_type=MESH_ID)
-
     class Ring:
-        def __init__(self, *what):
-            self.what = what
-            self.hold, self.p = what[2], what[3]
+        def __init__(self, level, kind, hold, p, along):
+            self.sem, self.hold, self.p = (level, kind), hold, p
+            self.right, self.left = along(1), along(3)
+            rows = hold.shape[1]
+            q = rows // 32 * 8
+            self.cut = [(0, rows - 3 * q)] + [(rows - k * q, q) for k in (3, 2, 1)]
+
+        def piece(self, source, k, sem, target):
+            rows = pl.ds(*self.cut[k])
+            slot = step(self.p, source)
+            return pltpu.make_async_remote_copy(
+                src_ref=self.hold.at[slot, rows], dst_ref=self.hold.at[slot, rows],
+                send_sem=send_sem.at[(*self.sem, sem)], recv_sem=recv_sem.at[(*self.sem, sem)],
+                device_id=target, device_id_type=MESH_ID)
 
         def start(self):
-            for by in (1, 3, 2):
-                copy(*self.what, by).start()
-
-        def arrived(self, by):
-            copy(*self.what, by, source=4 - by).wait_recv()
-            return step(self.p, 4 - by)
+            for k in range(4):
+                self.piece(0, k, k, self.right).start()
+                other = (k + 2) % 4
+                self.piece(0, other, 4 + other, self.left).start()
+
+        def relay(self):
+            for k in range(2):
+                self.piece(3, k, k, self.right).wait_recv()
+                self.piece(3, k, 8 + k, self.right).start()
+                self.piece(1, k + 2, 6 + k, self.left).wait_recv()
+                self.piece(1, k + 2, 10 + k, self.left).start()
+
+        def neighbours(self):
+            for k in range(2):
+                self.piece(3, k + 2, k + 2, self.right).wait_recv()
+                self.piece(1, k, 4 + k, self.left).wait_recv()
+            return step(self.p, 3), step(self.p, 1)
+
+        def across(self):
+            for k in range(2):
+                self.piece(2, k, 8 + k, self.right).wait_recv()
+                self.piece(2, k + 2, 10 + k, self.left).wait_recv()
+            return step(self.p, 2)
 
         def drain(self):
-            for by in (1, 3, 2):
-                copy(*self.what, by).wait_send()
+            for k in range(4):
+                self.piece(0, k, k, self.right).wait_send()
+                self.piece(0, k, 4 + k, self.left).wait_send()
+            for k in range(2):
+                self.piece(3, k, 8 + k, self.right).wait_send()
+                self.piece(1, k + 2, 10 + k, self.left).wait_send()
 
     mx, px = Ring(0, 0, map_x, x, along_x), Ring(0, 1, part_x, x, along_x)
     mz, pz = Ring(1, 0, map_z, z, along_z), Ring(1, 1, part_z, z, along_z)
@@ -212,7 +237,7 @@
         barrier = pltpu.get_barrier_semaphore()
         pl.semaphore_signal(barrier, inc=1, device_id=partner, device_id_type=MESH_ID)
         for along in (along_x, along_z, along_y):
-            for by in (1, 2, 3):
+            for by in (1, 3):
                 pl.semaphore_signal(barrier, inc=1, device_id=along(by), device_id_type=MESH_ID)
         noise[...] = jnp.zeros_like(noise)
         obs_var[...] = jnp.broadcast_to(var_ref[...] * 0.5, obs_var.shape[::-1]).T
@@ -220,7 +245,7 @@
         q = dot_nt(factor_ref[...], factor_ref[...])
         base[...] = q
         base_half[...] = q.astype(bf16)
-        pl.semaphore_wait(barrier, 10)
+        pl.semaphore_wait(barrier, 7)
         on_chip(own_map, pair_map, 0).start()
 
     fetch = pltpu.make_async_copy(maps_ref, maps_here, maps_sem.at[0])
@@ -234,6 +259,10 @@
     def _():
         map_x[x] = product(own_map[...], pair_map[...])
         mx.start()
+
+    @pl.when(jnp.logical_and(i == last, core == 0))
+    def _():
+        mx.relay()
 
     diagonal = eye(s)
     m = map_ref.shape[2]
@@ -295,10 +324,10 @@
     def total_part(ring, p):
         parts = ring.hold
         sum_ = moved(unpack(parts[p]), later[p])
-        left, right = ring.arrived(1), ring.arrived(3)
+        left, right = ring.neighbours()
         sum_ = sum_ + moved(unpack(parts[left]), later[left])
         sum_ = sum_ + moved(unpack(parts[right]), later[right])
-        across = ring.arrived(2)
+        across = ring.across()
         return pack(sum_ + moved(unpack(parts[across]), later[across]))
 
     def first_half():
@@ -322,35 +351,40 @@
 
     @pl.when(jnp.logical_and(i == last, core == 0))
     def _():
-        for by in (1, 3, 2):
-            mx.arrived(by)
-        x01, x23 = pairs(map_x)
-        map_z[z] = product(x01, x23)
-        mz.start()
         far = product(total_ref[1, :s], pair_map[...])
         mine = moved(first_half(), far) + moved(second_half(), pair_map[...])
         on_chip(own_part, pair_part, 1).wait_recv()
         part_x[x] = pack(mine + pair_part[...])
         px.start()
+        mx.neighbours()
+        mx.across()
+        x01, x23 = pairs(map_x)
+        map_z[z] = product(x01, x23)
+        mz.start()
         suffixes(map_x, x23)
+        px.relay()
         own_part[...] = moved(first_half(), total_ref[1, :s]) + second_half()
         on_chip(own_part, pair_part, 1).start()
+        mz.relay()
         before[0] = earlier_map(x, map_x, x01)
         part_z[z] = total_part(px, x)
         pz.start()
-        for by in (1, 3, 2):
-            mz.arrived(by)
+        mz.neighbours()
+        mz.across()
         z01, z23 = pairs(map_z)
         map_y[y] = product(z01, z23)
         my.start()
         suffixes(map_z, z23)
+        pz.relay()
         near = earlier_part(x, part_x, map_x)
+        my.relay()
         before[3] = product(earlier_map(z, map_z, z01), before[0])
         part_y[y] = total_part(pz, z)
         py.start()
         near = near + moved(earlier_part(z, part_z, map_z), before[0])
-        for by in (1, 3, 2):
-            my.arrived(by)
+        py.relay()
+        my.neighbours()
+        my.across()
         for q in (2, 1, 0):
             after = before[q + 1]
             before[q] = jnp.where(q < y, product(map_y[q], after), after)
@@ -362,10 +396,14 @@
         start_noise = dot_nn(u_hi_t, w_hi) + (dot_nn(u_hi_t, w_lo) + dot_nn(u_lo_t, w_hi))
         start_mean = product(jnp.broadcast_to(mean0_ref[...], (PAD, s)), t0)
         near = near + jnp.concatenate([start_noise, start_mean], axis=0)
-        for by in (1, 3, 2):
-            q = py.arrived(by)
+
+        def slab(q):
             part = moved(unpack(part_y[q]), before[jnp.minimum(q + 1, 3)])
-            near = near + jnp.where(q < y, part, 0.0)
+            return jnp.where(q < y, part, 0.0)
+
+        left, right = py.neighbours()
+        near = near + slab(left) + slab(right)
+        near = near + slab(py.across())
         state[...] = pack(near)
         on_chip(state, state, 2).start()
         entry[0] = near
@@ -389,10 +427,10 @@
                     t = h * half + k
                     maps = maps_here[h, k]
                     r = dot_nn(off[h], maps.astype(bf16)) + straight[h] * maps
-                    out_ref[pl.ds(t, 1), :] = (
+                    out_ref[1, pl.ds(t, 1), :] = (
                         jnp.sum(r * maps, axis=0, keepdims=True) + diag[pl.ds(t, 1), :]
                     )
-                    mean_ref[pl.ds(t, 1), :] = (
+                    out_ref[0, pl.ds(t, 1), :] = (
                         jnp.sum(first_mean[h] * maps, axis=0, keepdims=True)
                         + shift_ref[pl.ds(t, 1), :]
                     )
@@ -432,8 +470,8 @@
             pl.BlockSpec((count, s), whole),
             pl.BlockSpec(memory_space=pl.ANY),
         ],
-        out_specs=[pl.BlockSpec((count, s), whole)] * 2,
-        out_shape=[jax.ShapeDtypeStruct((count, s), f32)] * 2,
+        out_specs=pl.BlockSpec((2, count, s), three),
+        out_shape=jax.ShapeDtypeStruct((2, count, s), f32),
         scratch_shapes=[
             pltpu.VMEM((2, s, s), f32),
             pltpu.VMEM((m, 8), f32),
@@ -453,8 +491,8 @@
             pltpu.VMEM((2, s, s), bf16),
             pltpu.VMEM((2, s, s), f32),
             pltpu.VMEM((2, s, s), f32),
-            pltpu.SemaphoreType.DMA((3, 2, 3)),
-            pltpu.SemaphoreType.DMA((3, 2, 3)),
+            pltpu.SemaphoreType.DMA((3, 2, 12)),
+            pltpu.SemaphoreType.DMA((3, 2, 12)),
             pltpu.SemaphoreType.DMA((2, 3)),
             pltpu.SemaphoreType.DMA((1,)),
         ],
@@ -468,11 +506,11 @@
     init_mean, init_var, decay, coupling, obs_map, gain, noise_factor, obs_var, observed
 ):
     step_maps, maps, shift, total = local_maps(decay, coupling, obs_map, gain, observed)
-    means, variances = scan(
+    both = scan(
         decay, obs_var, noise_factor, obs_map, gain, step_maps, total, init_mean, init_var,
         shift, maps,
     )
-    return (means, variances)
+    return (both[0], both[1])
 
 
 def solution(mesh):

time: 72.8 us -> 69.3 us (0.952)
  Pallas kernels: 69.1 us -> 67 us
  local copies, waits for them, and re-layouts: 2.75 us -> 1.4 us
    unnamed x2 -> x0, local copies, waits for them, and re-layouts: 2.75 us -> none
    pallas_call x1, Pallas kernels: 56.3 us -> 54.2 us  [scan(): pl.pallas_call(functools.partial(scan_kernel, steps), grid=(count // (2 *...]
    squeeze x0 -> x1, local copies, waits for them, and re-layouts: none -> 1.4 us  [per_device(): return (both[0], both[1])]
where the time goes in v6:
time: 69.3 us; the launch traced here: 69.1 us
  Pallas kernels  67 us (97%)
  local copies, waits for them, and re-layouts  1.4 us (2%)
    pallas_call x1, Pallas kernels, scan(): pl.pallas_call(functools.partial(scan_kernel, steps), grid=(count // (2 *...  54.2 us
    pallas_call x1, Pallas kernels, local_maps(): pl.pallas_call(functools.partial(maps_kernel, steps), grid=(count // (2 *...  12.8 us
    squeeze x1, local copies, waits for them, and re-layouts, per_device(): return (both[0], both[1])  1.4 us

profile of v6, /device:TPU:1, one launch (start us, length us, event | category | flops | bytes accessed | tf_op | source)
XLA Modules:
  0.0 69.1 jit_solution(16135068385413112540)
XLA Ops:
  0.6 12.8 %local_maps.1 = (bf16[2,16,256,256]{3,2,1,0:T(8,128)(2,1)}, f32[2,16,256,256]{3,2,1,0:T(8,128)}, f32[32,256]{1,0:T(8,128)}, f32[2,272,256]{2,1,0:T(8,128)}) custom-call(f32[32,256]{1,0:T(8,128)} %decay_ref.3, f32[32,64]{1,0:T(8,128)} %observed_ref.1, bf16[2,16,256,256]{3,2,1,0:T(8,128)(2,1)} %bitcast.10, bf16[2,16,64,256]{3,2,1,0:T(8,128)(2,1)} %bitcast.11, ...), custom_call_target="tpu_custom_call" | custom-call | tf_op jit(solution)/shard_map/local_maps/pallas_call | solution.py:131
  13.4 54.2 %scan_devices.1 = f32[2,32,256]{2,1,0:T(8,128)} custom-call(f32[32,256]{1,0:T(8,128)} %decay_ref.3, f32[1,64]{1,0:T(1,128)} %bitcast.17, bf16[256,256]{1,0:T(8,128)(2,1)} %factor_ref.1, bf16[2,16,64,256]{3,2,1,0:T(8,128)(2,1)} %bitcast.12, bf16[2,16,64,256]{3,2,1,0:T(8,128)(2,1)} %bitcast.14, bf16[2,16,256,256]{3,2,1,0:T(8,128)(2,1)} %get-tuple-element.6.step_ref, ...), custom_call_target="tpu_custom_call" | custom-call | tf_op jit(solution)/shard_map/scan_devices/pallas_call | solution.py:457
  67.7 1.4 %slice_bitcast_fusion = (f32[32,256]{1,0:T(8,128)}, f32[32,256]{1,0:T(8,128)}) fusion(f32[2,32,256]{2,1,0:T(8,128)} %scan_devices.1), kind=kLoop, calls=%fused_computation | loop fusion | bytes 131072 | tf_op jit(solution)/shard_map/squeeze | solution.py:513

commit v7 on v6

--- a/solution.py
+++ b/solution.py
@@ -11,6 +11,7 @@
 bf16 = jnp.bfloat16
 PAD = 16
 SPB = 4
+SPN = 8
 
 
 def dot_nn(a, b):
@@ -255,14 +256,10 @@
         fetch.start()
         on_chip(own_map, pair_map, 0).wait_recv()
 
-    @pl.when(jnp.logical_and(i == 1, core == 0))
-    def _():
-        map_x[x] = product(own_map[...], pair_map[...])
+    @pl.when(jnp.logical_and(i == 1, core == 1))
+    def _():
+        map_x[x] = product(pair_map[...], own_map[...])
         mx.start()
-
-    @pl.when(jnp.logical_and(i == last, core == 0))
-    def _():
-        mx.relay()
 
     diagonal = eye(s)
     m = map_ref.shape[2]
@@ -283,12 +280,13 @@
     ns = [noise[0], noise[1]]
     ready = [build(0, 0), build(1, 0)]
     for j in range(steps):
+        now = ready
+        vs = [ns[h] * now[h][1] + dot_nt(ns[h].astype(bf16), step_ref[h, j]) for h in range(2)]
+        if j + 1 < steps:
+            ready = [build(0, j + 1), build(1, j + 1)]
         for h in range(2):
-            t, decay, decay_t, left, right = ready[h]
-            e = step_ref[h, j]
-            v = ns[h] * decay + dot_nt(ns[h].astype(bf16), e)
-            if j + 1 < steps:
-                ready[h] = build(h, j + 1)
+            t, decay, decay_t, left, right = now[h]
+            e, v = step_ref[h, j], vs[h]
             pushed = dot_nn(jnp.concatenate([e, left], axis=1),
                             jnp.concatenate([v.astype(bf16), right], axis=0))
             n = v * decay_t + base[...] + pushed
@@ -340,10 +338,28 @@
     def _():
         own_part[...] = moved(first_half(), total_ref[1, :s]) + second_half()
         on_chip(own_part, pair_part, 1).start()
+        mx.relay()
         before[0] = product(pair_map[...], total_ref[0, :s])
+        mx.neighbours()
+        mx.across()
+        on_chip(map_x, map_x, 3).start()
+        x01, x23 = pairs(map_x)
+        map_z[z] = product(x01, x23)
+        mz.start()
+        mz.relay()
+        mz.neighbours()
+        mz.across()
+        on_chip(map_z, map_z, 4).start()
+        z01, z23 = pairs(map_z)
+        map_y[y] = product(z01, z23)
+        my.start()
         on_chip(own_part, pair_part, 1).wait_recv()
         part = pair_part[...]
         kept = moved(part, total_ref[0, :s]) + first_half()
+        my.relay()
+        my.neighbours()
+        my.across()
+        on_chip(map_y, map_y, 5).start()
         on_chip(state, state, 2).wait_recv()
         near = unpack(state[...])
         entry[0] = moved(near, pair_map[...]) + pair_part[...]
@@ -356,35 +372,26 @@
         on_chip(own_part, pair_part, 1).wait_recv()
         part_x[x] = pack(mine + pair_part[...])
         px.start()
-        mx.neighbours()
-        mx.across()
-        x01, x23 = pairs(map_x)
-        map_z[z] = product(x01, x23)
-        mz.start()
-        suffixes(map_x, x23)
-        px.relay()
         own_part[...] = moved(first_half(), total_ref[1, :s]) + second_half()
         on_chip(own_part, pair_part, 1).start()
-        mz.relay()
+        px.relay()
+        on_chip(map_x, map_x, 3).wait_recv()
+        x01, x23 = pairs(map_x)
+        suffixes(map_x, x23)
         before[0] = earlier_map(x, map_x, x01)
         part_z[z] = total_part(px, x)
         pz.start()
-        mz.neighbours()
-        mz.across()
+        near = earlier_part(x, part_x, map_x)
+        pz.relay()
+        on_chip(map_z, map_z, 4).wait_recv()
         z01, z23 = pairs(map_z)
-        map_y[y] = product(z01, z23)
-        my.start()
         suffixes(map_z, z23)
-        pz.relay()
-        near = earlier_part(x, part_x, map_x)
-        my.relay()
         before[3] = product(earlier_map(z, map_z, z01), before[0])
         part_y[y] = total_part(pz, z)
         py.start()
         near = near + moved(earlier_part(z, part_z, map_z), before[0])
         py.relay()
-        my.neighbours()
-        my.across()
+        on_chip(map_y, map_y, 5).wait_recv()
         for q in (2, 1, 0):
             after = before[q + 1]
             before[q] = jnp.where(q < y, product(map_y[q], after), after)
@@ -419,11 +426,11 @@
             first_mean[h] = jnp.broadcast_to(entry[h, s:s + 8].T[:, 0:1], (s, s))
         fetch.wait()
 
-        @pl.loop(0, half // steps)
+        @pl.loop(0, half // 4)
         def _(block):
-            for j in range(steps):
+            for j in range(4):
                 for h in range(2):
-                    k = block * steps + j
+                    k = block * 4 + j
                     t = h * half + k
                     maps = maps_here[h, k]
                     r = dot_nn(off[h], maps.astype(bf16)) + straight[h] * maps
@@ -440,15 +447,22 @@
 
     @pl.when(jnp.logical_and(i == last, core == 0))
     def _():
-        for ring in (mx, px, mz, pz, my, py):
+        for ring in (px, pz, py):
             ring.drain()
         on_chip(state, state, 2).wait_send()
+
+    @pl.when(jnp.logical_and(i == last, core == 1))
+    def _():
+        for ring in (mx, mz, my):
+            ring.drain()
+        for k, hold in ((3, map_x), (4, map_z), (5, map_y)):
+            on_chip(hold, hold, k).wait_send()
 
 
 def scan(decay, obs_var, factor, obs_map, gain, step_maps, total, init_mean, init_var, shift, maps):
     count, s = decay.shape
     m = obs_map.shape[1]
-    steps = SPB
+    steps = SPN
     rows = s + PAD
     packed = s // 2 + s // 4 + 8
     block = lambda i: (0, i, 0, 0)
@@ -493,7 +507,7 @@
             pltpu.VMEM((2, s, s), f32),
             pltpu.SemaphoreType.DMA((3, 2, 12)),
             pltpu.SemaphoreType.DMA((3, 2, 12)),
-            pltpu.SemaphoreType.DMA((2, 3)),
+            pltpu.SemaphoreType.DMA((2, 6)),
             pltpu.SemaphoreType.DMA((1,)),
         ],
         compiler_params=pltpu.CompilerParams(collective_id=0, has_side_effects=True),

time: 69.3 us -> 66.2 us (0.955)
  Pallas kernels: 67 us -> 63.9 us
    pallas_call x1, Pallas kernels: 54.2 us -> 51.1 us  [scan(): pl.pallas_call(functools.partial(scan_kernel, steps), grid=(count // (2 *...]
where the time goes in v7:
time: 66.2 us; the launch traced here: 65.9 us
  Pallas kernels  63.9 us (97%)
  local copies, waits for them, and re-layouts  1.4 us (2%)
    pallas_call x1, Pallas kernels, scan(): pl.pallas_call(functools.partial(scan_kernel, steps), grid=(count // (2 *...  51.1 us
    pallas_call x1, Pallas kernels, local_maps(): pl.pallas_call(functools.partial(maps_kernel, steps), grid=(count // (2 *...  12.8 us
    squeeze x1, local copies, waits for them, and re-layouts, per_device(): return (both[0], both[1])  1.4 us

profile of v7, /device:TPU:1, one launch (start us, length us, event | category | flops | bytes accessed | tf_op | source)
XLA Modules:
  0.0 65.9 jit_solution(13498439160715745795)
XLA Ops:
  0.6 12.8 %local_maps.1 = (bf16[2,16,256,256]{3,2,1,0:T(8,128)(2,1)}, f32[2,16,256,256]{3,2,1,0:T(8,128)}, f32[32,256]{1,0:T(8,128)}, f32[2,272,256]{2,1,0:T(8,128)}) custom-call(f32[32,256]{1,0:T(8,128)} %decay_ref.3, f32[32,64]{1,0:T(8,128)} %observed_ref.1, bf16[2,16,256,256]{3,2,1,0:T(8,128)(2,1)} %bitcast.10, bf16[2,16,64,256]{3,2,1,0:T(8,128)(2,1)} %bitcast.11, ...), custom_call_target="tpu_custom_call" | custom-call | tf_op jit(solution)/shard_map/local_maps/pallas_call | solution.py:132
  13.4 51.1 %scan_devices.1 = f32[2,32,256]{2,1,0:T(8,128)} custom-call(f32[32,256]{1,0:T(8,128)} %decay_ref.3, f32[1,64]{1,0:T(1,128)} %bitcast.17, bf16[256,256]{1,0:T(8,128)(2,1)} %factor_ref.1, bf16[2,16,64,256]{3,2,1,0:T(8,128)(2,1)} %bitcast.12, bf16[2,16,64,256]{3,2,1,0:T(8,128)(2,1)} %bitcast.14, bf16[2,16,256,256]{3,2,1,0:T(8,128)(2,1)} %get-tuple-element.6.step_ref, ...), custom_call_target="tpu_custom_call" | custom-call | tf_op jit(solution)/shard_map/scan_devices/pallas_call | solution.py:471
  64.5 1.4 %slice_bitcast_fusion = (f32[32,256]{1,0:T(8,128)}, f32[32,256]{1,0:T(8,128)}) fusion(f32[2,32,256]{2,1,0:T(8,128)} %scan_devices.1), kind=kLoop, calls=%fused_computation | loop fusion | bytes 131072 | tf_op jit(solution)/shard_map/squeeze | solution.py:527

commit v8 on v7

--- a/solution.py
+++ b/solution.py
@@ -70,7 +70,7 @@
 
 
 def maps_kernel(steps, decay_ref, observed_ref, coupling_ref, map_ref, gain_ref,
-                step_ref, maps_ref, shift_ref, total_ref, state):
+                step_ref, maps_ref, shift_ref, total_ref, own_ref, state):
     i = pl.program_id(0)
     s = decay_ref.shape[1]
     half = decay_ref.shape[0] // 2
@@ -92,6 +92,7 @@
         both = dot_nn(jnp.concatenate([z_hi, z_lo], axis=0), gain)
         return t, decay, e_hi, e_lo, both[:PAD] + both[PAD:]
 
+    diagonal = eye(s)
     maps = [state[0], state[1]]
     ready = [build(0, 0), build(1, 0)]
     for j in range(steps):
@@ -102,6 +103,7 @@
             y = maps[h] * decay + (moved[:s + PAD] + (moved[s + PAD:] + dot_nt(m_hi, e_lo)))
             b = y[s:] + shift
             maps_ref[h, j] = y[:s]
+            own_ref[pl.ds(t, 1), :] = jnp.sum(jnp.where(diagonal, y[:s], 0.0), axis=0, keepdims=True)
             shift_ref[pl.ds(t, 1), :] = b[0:1]
             maps[h] = jnp.concatenate([y[:s], b], axis=0)
             if j + 1 < steps:
@@ -135,12 +137,14 @@
         in_specs=[pl.BlockSpec((count, s), whole), pl.BlockSpec((count, m), whole),
                   square, flat, flat],
         out_specs=[square, square, pl.BlockSpec((count, s), whole),
-                   pl.BlockSpec((2, s + PAD, s), lambda i: (0, 0, 0))],
+                   pl.BlockSpec((2, s + PAD, s), lambda i: (0, 0, 0)),
+                   pl.BlockSpec((count, s), whole)],
         out_shape=[
             jax.ShapeDtypeStruct((2, count // 2, s, s), bf16),
             jax.ShapeDtypeStruct((2, count // 2, s, s), f32),
             jax.ShapeDtypeStruct((count, s), f32),
             jax.ShapeDtypeStruct((2, s + PAD, s), f32),
+            jax.ShapeDtypeStruct((count, s), f32),
         ],
         scratch_shapes=[pltpu.VMEM((2, s + PAD, s), f32)],
         name="local_maps",
@@ -148,10 +152,10 @@
 
 
 def scan_kernel(steps, decay_ref, var_ref, factor_ref, map_ref, gain_ref, step_ref, total_ref,
-                mean0_ref, var0_ref, shift_ref, maps_ref, out_ref,
+                mean0_ref, var0_ref, shift_ref, own_ref, maps_ref, out_ref,
                 noise, obs_var, base, base_half, diag, own_map, own_part,
                 map_x, map_z, map_y, part_x, part_z, part_y,
-                later, before, pair_map, pair_part, state, entry, maps_here, off, straight,
+                later, before, pair_map, pair_part, state, entry, maps_here, cov_half,
                 first_mean, send_sem, recv_sem, pair_sem, maps_sem):
     i = pl.program_id(0)
     last = pl.num_programs(0) - 1
@@ -418,12 +422,13 @@
 
     @pl.when(i == last)
     def _():
+        firsts = []
         for h in range(2):
-            cov = entry[h, :s]
-            off[h] = jnp.where(diagonal, 0.0, cov).astype(bf16)
-            held = jnp.sum(jnp.where(diagonal, cov, 0.0), axis=1, keepdims=True)
-            straight[h] = jnp.broadcast_to(held, (s, s))
-            first_mean[h] = jnp.broadcast_to(entry[h, s:s + 8].T[:, 0:1], (s, s))
+            cov, mean = entry[h, :s], entry[h, s:]
+            held = jnp.sum(jnp.where(diagonal, cov, 0.0), axis=0, keepdims=True)
+            cov_half[h] = cov.astype(bf16)
+            first_mean[h] = jnp.broadcast_to(mean[:8].T[:, 0:1], (s, s))
+            firsts.append((held, held.astype(bf16).astype(f32)))
         fetch.wait()
 
         @pl.loop(0, half // 4)
@@ -433,9 +438,14 @@
                     k = block * 4 + j
                     t = h * half + k
                     maps = maps_here[h, k]
-                    r = dot_nn(off[h], maps.astype(bf16)) + straight[h] * maps
+                    near_maps = maps.astype(bf16)
+                    r = dot_nn(cov_half[h], near_maps)
+                    held, held_hi = firsts[h]
+                    own = own_ref[pl.ds(t, 1), :]
+                    own_hi = own.astype(bf16).astype(f32)
                     out_ref[1, pl.ds(t, 1), :] = (
-                        jnp.sum(r * maps, axis=0, keepdims=True) + diag[pl.ds(t, 1), :]
+                        jnp.sum(r * maps, axis=0, keepdims=True)
+                        + own * (held * own - held_hi * own_hi) + diag[pl.ds(t, 1), :]
                     )
                     out_ref[0, pl.ds(t, 1), :] = (
                         jnp.sum(first_mean[h] * maps, axis=0, keepdims=True)
@@ -459,7 +469,8 @@
             on_chip(hold, hold, k).wait_send()
 
 
-def scan(decay, obs_var, factor, obs_map, gain, step_maps, total, init_mean, init_var, shift, maps):
+def scan(decay, obs_var, factor, obs_map, gain, step_maps, total, init_mean, init_var, shift, own,
+         maps):
     count, s = decay.shape
     m = obs_map.shape[1]
     steps = SPN
@@ -481,6 +492,7 @@
             pl.BlockSpec((2, rows, s), three),
             pl.BlockSpec((1, s), whole),
             pl.BlockSpec((1, s), whole),
+            pl.BlockSpec((count, s), whole),
             pl.BlockSpec((count, s), whole),
             pl.BlockSpec(memory_space=pl.ANY),
         ],
@@ -504,7 +516,6 @@
             pltpu.VMEM((2, count // 2, s, s), f32),
             pltpu.VMEM((2, s, s), bf16),
             pltpu.VMEM((2, s, s), f32),
-            pltpu.VMEM((2, s, s), f32),
             pltpu.SemaphoreType.DMA((3, 2, 12)),
             pltpu.SemaphoreType.DMA((3, 2, 12)),
             pltpu.SemaphoreType.DMA((2, 6)),
@@ -513,16 +524,16 @@
         compiler_params=pltpu.CompilerParams(collective_id=0, has_side_effects=True),
         name="scan_devices",
     )(decay, obs_var[None, :], factor, halves(obs_map), halves(gain), step_maps, total,
-      init_mean[None, :], init_var[None, :], shift, maps)
+      init_mean[None, :], init_var[None, :], shift, own, maps)
 
 
 def per_device(
     init_mean, init_var, decay, coupling, obs_map, gain, noise_factor, obs_var, observed
 ):
-    step_maps, maps, shift, total = local_maps(decay, coupling, obs_map, gain, observed)
+    step_maps, maps, shift, total, own = local_maps(decay, coupling, obs_map, gain, observed)
     both = scan(
         decay, obs_var, noise_factor, obs_map, gain, step_maps, total, init_mean, init_var,
-        shift, maps,
+        shift, own, maps,
     )
     return (both[0], both[1])
 

time: 66.2 us -> 65.9 us (level)
  no operation moved by 1% of the time
where the time goes in v8:
time: 65.9 us; the launch traced here: 65.6 us
  Pallas kernels  63.5 us (96%)
  local copies, waits for them, and re-layouts  1.4 us (2%)
    pallas_call x1, Pallas kernels, scan(): pl.pallas_call(functools.partial(scan_kernel, steps), grid=(count // (2 *...  50.8 us
    pallas_call x1, Pallas kernels, local_maps(): pl.pallas_call(functools.partial(maps_kernel, steps), grid=(count // (2 *...  12.8 us
    squeeze x1, local copies, waits for them, and re-layouts, per_device(): return (both[0], both[1])  1.4 us

profile of v8, /device:TPU:1, one launch (start us, length us, event | category | flops | bytes accessed | tf_op | source)
XLA Modules:
  0.0 65.6 jit_solution(530389205145908760)
XLA Ops:
  0.6 12.8 %local_maps.1 = (bf16[2,16,256,256]{3,2,1,0:T(8,128)(2,1)}, f32[2,16,256,256]{3,2,1,0:T(8,128)}, f32[32,256]{1,0:T(8,128)}, f32[2,272,256]{2,1,0:T(8,128)}, f32[32,256]{1,0:T(8,128)}) custom-call(f32[32,256]{1,0:T(8,128)} %decay_ref.3, f32[32,64]{1,0:T(8,128)} %observed_ref.1, bf16[2,16,256,256]{3,2,1,0:T(8,128)(2,1)} %bitcast.10, ...), custom_call_target="tpu_custom_call" | custom-call | tf_op jit(solution)/shard_map/local_maps/pallas_call | solution.py:134
  13.4 50.8 %scan_devices.1 = f32[2,32,256]{2,1,0:T(8,128)} custom-call(f32[32,256]{1,0:T(8,128)} %decay_ref.3, f32[1,64]{1,0:T(1,128)} %bitcast.17, bf16[256,256]{1,0:T(8,128)(2,1)} %factor_ref.1, bf16[2,16,64,256]{3,2,1,0:T(8,128)(2,1)} %bitcast.12, bf16[2,16,64,256]{3,2,1,0:T(8,128)(2,1)} %bitcast.14, bf16[2,16,256,256]{3,2,1,0:T(8,128)(2,1)} %get-tuple-element.7.step_ref, ...), custom_call_target="tpu_custom_call" | custom-call | tf_op jit(solution)/shard_map/scan_devices/pallas_call | solution.py:482
  64.2 1.4 %slice_bitcast_fusion = (f32[32,256]{1,0:T(8,128)}, f32[32,256]{1,0:T(8,128)}) fusion(f32[2,32,256]{2,1,0:T(8,128)} %scan_devices.1), kind=kLoop, calls=%fused_computation | loop fusion | bytes 131072 | tf_op jit(solution)/shard_map/squeeze | solution.py:538
